TPU v7x, 256 devices: a whole 4x4x8 slice. The times are simulated.
256 devices in a mesh: depth: 16 (over z, y_lo), freq: 16 (over y_hi, x, core).
Axes of the slice: x: 4, y: 4 (y_hi: 2, y_lo: 2; y = y_hi * 2 + y_lo), z: 8, core: 2. Of those that a mesh axis runs over, the one named last changes fastest.
Arguments:
- extrap: bfloat16 [16, 16, 2, 1024, 1024], P('depth', 'freq'), may hold values from -0.125 to 0.125
- source_field: bfloat16 [16, 128, 2, 1024], P('freq'), may hold values from -6 to 6
- record_field: bfloat16 [16, 128, 2, 1024], P('freq'), may hold values from -6 to 6
- shot_of_record: int32 [128], replicated, may hold values from 0 to 127, each once
- freq_index: int32 [16], P('freq'), may hold values from 0 to 127, as said below
- angle_lag: int32 [1024, 256], replicated, may hold values from 0 to 15
Outputs:
- gathers: float32 [1024, 16, 256], P(('freq', 'depth'))
Inputs may be any that keep to these rules, and one draw needn't show every extreme that they name: `shot_of_record`: each shot is named once. `freq_index`: the frequency numbers are distinct, and the largest one, 127, is always held by some slot.
All inputs are finite; a program needn't handle non-finite values.
Results may differ from a plain program's by a relative error of at most 0.035.
Values may be sent and summed in bfloat16 or wider, within the bound.
A program may use at most 64 MiB of HBM per device.

v0:
```python
import math

import jax
import jax.numpy as jnp
from jax import lax
from jax.sharding import PartitionSpec as P


def from_behind(value, axis, steps):
    count = lax.axis_size(axis)
    leading, last = (max(0, -steps), min(count, count - steps))
    return lax.ppermute(value, axis, [(source, source + steps) for source in range(leading, last)])


def make_block(real_part, imag_part):
    upper = jnp.concatenate([real_part, imag_part], axis=1)
    lower = jnp.concatenate([-imag_part, real_part], axis=1)
    return jnp.concatenate([upper, lower], axis=0)


def shards(extrap, source_field, record_field, shot_of_record, freq_index, angle_lag):
    segment_index = lax.axis_index("depth")
    depth_count = lax.axis_size("depth")
    freq_count = lax.axis_size("freq")
    points = source_field.shape[3]
    shot_count = source_field.shape[1]
    extrapolator = make_block(extrap[0, 0, 0], extrap[0, 0, 1])
    paired = jnp.take(source_field[0].reshape(shot_count, 2 * points), shot_of_record, axis=0)
    record_rows = jnp.concatenate([record_field[0, :, 1], record_field[0, :, 0]], axis=1)
    batch_count = 1
    batch_rows = shot_count // batch_count
    inputs = jnp.concatenate(
        [
            paired.reshape(batch_count, batch_rows, 2 * points),
            record_rows.reshape(batch_count, batch_rows, 2 * points),
        ],
        axis=1,
    )

    def extend(values):
        return jnp.dot(values, extrapolator, preferred_element_type=jnp.float32).astype(
            jnp.bfloat16
        )

    def vacant(values):
        return jnp.zeros_like(values)

    def advance(tick_index, state_pair):
        arrived, finished = state_pair
        batch_slot = tick_index - segment_index
        active = (batch_slot >= 0) & (batch_slot < batch_count)
        slot_clamped = jnp.clip(batch_slot, 0, batch_count - 1)
        incoming = lax.dynamic_index_in_dim(inputs, slot_clamped, 0, keepdims=False)
        entering = jnp.where(segment_index == 0, incoming, arrived)
        advanced = lax.cond(active, extend, vacant, entering)
        previous = lax.dynamic_index_in_dim(finished, slot_clamped, 0, keepdims=False)
        finished = lax.dynamic_update_index_in_dim(
            finished, jnp.where(active, advanced, previous), slot_clamped, 0
        )
        arrived = from_behind(advanced, "depth", 1)
        return (arrived, finished)

    start_state = (jnp.zeros((2 * batch_rows, 2 * points), jnp.bfloat16), jnp.zeros_like(inputs))
    arrived, finished = lax.fori_loop(0, batch_count + depth_count - 1, advance, start_state)
    source_stack = finished[:, :batch_rows].reshape(2 * shot_count, points)
    record_stack = (
        finished[:, batch_rows:]
        .reshape(shot_count, 2, points)[:, ::-1]
        .reshape(2 * shot_count, points)
    )
    factor = (
        (freq_index[0].astype(jnp.float32) + 1.0)
        / (8 * freq_count)
        / math.sqrt(shot_count * freq_count)
    )
    partial_value = lax.dot_general(
        source_stack, record_stack, (((0,), (0,)), ((), ())), preferred_element_type=jnp.float32
    )
    image_panel = lax.psum_scatter(
        (partial_value * factor).astype(jnp.bfloat16), "freq", scatter_dimension=0, tiled=True
    )
    gathered = lax.all_to_all(
        image_panel[:, None, :], "depth", split_axis=0, concat_axis=1, tiled=True
    )
    row_count = gathered.shape[0]
    padded = jnp.concatenate([gathered, jnp.zeros_like(gathered)], axis=1)

    def add_lagged(lag_value, stacked_sum):
        shifted = lax.dynamic_slice_in_dim(padded, lag_value, depth_count, 1).reshape(
            row_count * depth_count, points
        )
        selector = (angle_lag == lag_value).astype(jnp.bfloat16)
        return stacked_sum + jnp.dot(shifted, selector, preferred_element_type=jnp.float32)

    stacked_sum = lax.fori_loop(
        0,
        depth_count,
        add_lagged,
        jnp.zeros((row_count * depth_count, angle_lag.shape[1]), jnp.float32),
    )
    return (stacked_sum / math.sqrt(points)).reshape(row_count, depth_count, angle_lag.shape[1])


def solution(mesh):
    placed = (
        P("depth", "freq", None, None, None),
        P("freq", None, None, None),
        P("freq", None, None, None),
        P(),
        P("freq"),
        P(),
    )
    return jax.shard_map(
        shards,
        mesh=mesh,
        in_specs=placed,
        out_specs=P(("freq", "depth"), None, None),
        check_vma=False,
    )
```

profile of v0, /device:TPU:32, one launch (start us, length us, event | category | flops | bytes accessed | tf_op | source)
XLA Modules:
  0.0 612.3 jit_solution(9860138409034158853)
XLA Ops:
  20.8 23.7 %maximum_maximum_fusion = bf16[2048,2048]{1,0:T(8,128)(2,1)} fusion(bf16[1024,1024]{1,0:T(8,128)(2,1)} %get-tuple-element.289, bf16[1024,1024]{1,0:T(8,128)(2,1)S(1)} %fusion.4, bf16[1024,1024]{1,0:T(8,128)(2,1)S(1)} %copy-done.2), kind=kLoop, calls=%fused_computation.10 | loop fusion | flops 33554432 | bytes 14680064 | tf_op jit(solution)/shard_map/concatenate | solution.py:18
  45.8 397.1 %while.30 = (s32[]{:T(128)}, bf16[256,2048]{1,0:T(8,128)(2,1)}, bf16[1,256,2048]{2,1,0:T(8,128)(2,1)S(1)}, s32[]{:T(128)}, pred[]{:T(512)}, /*index=5*/bf16[1,25...) while((s32[]{:T(128)}, bf16[256,2048]{1,0:T(8,128)(2,1)}, ...), condition=%wide.region_3.4_spmd, body=%wide.region_0.3_spmd.sunk | while | flops 2149056512 | bytes 18874580 | solution.py:64
  49.7 24.0 %collective-permute-done = bf16[256,2048]{1,0:T(8,128)(2,1)} collective-permute-done((bf16[256,2048]{1,0:T(8,128)(2,1)S(1)}, bf16[256,2048]{1,0:T(8,128)(2,1)}, u32[]{:S(2)}, u32[]{:S(2)}) %collective-permute-start) | collective-permute-done | bytes 1048608 | tf_op jit(solution)/shard_map/while/body/eval_jaxpr/ppermute | solution.py:12
  76.7 28.2 %collective-permute-done = bf16[256,2048]{1,0:T(8,128)(2,1)} collective-permute-done((bf16[256,2048]{1,0:T(8,128)(2,1)S(1)}, bf16[256,2048]{1,0:T(8,128)(2,1)}, u32[]{:S(2)}, u32[]{:S(2)}) %collective-permute-start) | collective-permute-done | bytes 1048608 | tf_op jit(solution)/shard_map/while/body/eval_jaxpr/ppermute | solution.py:12
  113.2 21.9 %collective-permute-done = bf16[256,2048]{1,0:T(8,128)(2,1)} collective-permute-done((bf16[256,2048]{1,0:T(8,128)(2,1)S(1)}, bf16[256,2048]{1,0:T(8,128)(2,1)}, u32[]{:S(2)}, u32[]{:S(2)}) %collective-permute-start) | collective-permute-done | bytes 1048608 | tf_op jit(solution)/shard_map/while/body/eval_jaxpr/ppermute | solution.py:12
  142.8 18.4 %collective-permute-done = bf16[256,2048]{1,0:T(8,128)(2,1)} collective-permute-done((bf16[256,2048]{1,0:T(8,128)(2,1)S(1)}, bf16[256,2048]{1,0:T(8,128)(2,1)}, u32[]{:S(2)}, u32[]{:S(2)}) %collective-permute-start) | collective-permute-done | bytes 1048608 | tf_op jit(solution)/shard_map/while/body/eval_jaxpr/ppermute | solution.py:12
  166.1 18.2 %collective-permute-done = bf16[256,2048]{1,0:T(8,128)(2,1)} collective-permute-done((bf16[256,2048]{1,0:T(8,128)(2,1)S(1)}, bf16[256,2048]{1,0:T(8,128)(2,1)}, u32[]{:S(2)}, u32[]{:S(2)}) %collective-permute-start) | collective-permute-done | bytes 1048608 | tf_op jit(solution)/shard_map/while/body/eval_jaxpr/ppermute | solution.py:12
  184.4 7.8 %collective-permute-start = (bf16[256,2048]{1,0:T(8,128)(2,1)S(1)}, bf16[256,2048]{1,0:T(8,128)(2,1)}, u32[]{:S(2)}, u32[]{:S(2)}) collective-permute-start(bf16[256,2048]{1,0:T(8,128)(2,1)S(1)} %get-tuple-element.409), channel_id=1, source_target_pairs={{0,16},{16,32},{32,48},{48,64},{64,80},{80,96},{96,112},{112,128},... | collective-permute-start | bytes 3145736 | tf_op jit(solution)/shard_map/while/body/eval_jaxpr/ppermute | solution.py:12
  192.5 17.0 %collective-permute-done = bf16[256,2048]{1,0:T(8,128)(2,1)} collective-permute-done((bf16[256,2048]{1,0:T(8,128)(2,1)S(1)}, bf16[256,2048]{1,0:T(8,128)(2,1)}, u32[]{:S(2)}, u32[]{:S(2)}) %collective-permute-start) | collective-permute-done | bytes 1048608 | tf_op jit(solution)/shard_map/while/body/eval_jaxpr/ppermute | solution.py:12
  214.7 18.4 %collective-permute-done = bf16[256,2048]{1,0:T(8,128)(2,1)} collective-permute-done((bf16[256,2048]{1,0:T(8,128)(2,1)S(1)}, bf16[256,2048]{1,0:T(8,128)(2,1)}, u32[]{:S(2)}, u32[]{:S(2)}) %collective-permute-start) | collective-permute-done | bytes 1048608 | tf_op jit(solution)/shard_map/while/body/eval_jaxpr/ppermute | solution.py:12
  239.1 15.3 %collective-permute-done = bf16[256,2048]{1,0:T(8,128)(2,1)} collective-permute-done((bf16[256,2048]{1,0:T(8,128)(2,1)S(1)}, bf16[256,2048]{1,0:T(8,128)(2,1)}, u32[]{:S(2)}, u32[]{:S(2)}) %collective-permute-start) | collective-permute-done | bytes 1048608 | tf_op jit(solution)/shard_map/while/body/eval_jaxpr/ppermute | solution.py:12
  254.6 7.6 %collective-permute-start = (bf16[256,2048]{1,0:T(8,128)(2,1)S(1)}, bf16[256,2048]{1,0:T(8,128)(2,1)}, u32[]{:S(2)}, u32[]{:S(2)}) collective-permute-start(bf16[256,2048]{1,0:T(8,128)(2,1)S(1)} %get-tuple-element.409), channel_id=1, source_target_pairs={{0,16},{16,32},{32,48},{48,64},{64,80},{80,96},{96,112},{112,128},... | collective-permute-start | bytes 3145736 | tf_op jit(solution)/shard_map/while/body/eval_jaxpr/ppermute | solution.py:12
  262.5 15.7 %collective-permute-done = bf16[256,2048]{1,0:T(8,128)(2,1)} collective-permute-done((bf16[256,2048]{1,0:T(8,128)(2,1)S(1)}, bf16[256,2048]{1,0:T(8,128)(2,1)}, u32[]{:S(2)}, u32[]{:S(2)}) %collective-permute-start) | collective-permute-done | bytes 1048608 | tf_op jit(solution)/shard_map/while/body/eval_jaxpr/ppermute | solution.py:12
  285.1 17.7 %collective-permute-done = bf16[256,2048]{1,0:T(8,128)(2,1)} collective-permute-done((bf16[256,2048]{1,0:T(8,128)(2,1)S(1)}, bf16[256,2048]{1,0:T(8,128)(2,1)}, u32[]{:S(2)}, u32[]{:S(2)}) %collective-permute-start) | collective-permute-done | bytes 1048608 | tf_op jit(solution)/shard_map/while/body/eval_jaxpr/ppermute | solution.py:12
  308.5 16.6 %collective-permute-done = bf16[256,2048]{1,0:T(8,128)(2,1)} collective-permute-done((bf16[256,2048]{1,0:T(8,128)(2,1)S(1)}, bf16[256,2048]{1,0:T(8,128)(2,1)}, u32[]{:S(2)}, u32[]{:S(2)}) %collective-permute-start) | collective-permute-done | bytes 1048608 | tf_op jit(solution)/shard_map/while/body/eval_jaxpr/ppermute | solution.py:12
  331.8 16.3 %collective-permute-done = bf16[256,2048]{1,0:T(8,128)(2,1)} collective-permute-done((bf16[256,2048]{1,0:T(8,128)(2,1)S(1)}, bf16[256,2048]{1,0:T(8,128)(2,1)}, u32[]{:S(2)}, u32[]{:S(2)}) %collective-permute-start) | collective-permute-done | bytes 1048608 | tf_op jit(solution)/shard_map/while/body/eval_jaxpr/ppermute | solution.py:12
  354.6 16.8 %collective-permute-done = bf16[256,2048]{1,0:T(8,128)(2,1)} collective-permute-done((bf16[256,2048]{1,0:T(8,128)(2,1)S(1)}, bf16[256,2048]{1,0:T(8,128)(2,1)}, u32[]{:S(2)}, u32[]{:S(2)}) %collective-permute-start) | collective-permute-done | bytes 1048608 | tf_op jit(solution)/shard_map/while/body/eval_jaxpr/ppermute | solution.py:12
  379.1 17.5 %collective-permute-done = bf16[256,2048]{1,0:T(8,128)(2,1)} collective-permute-done((bf16[256,2048]{1,0:T(8,128)(2,1)S(1)}, bf16[256,2048]{1,0:T(8,128)(2,1)}, u32[]{:S(2)}, u32[]{:S(2)}) %collective-permute-start) | collective-permute-done | bytes 1048608 | tf_op jit(solution)/shard_map/while/body/eval_jaxpr/ppermute | solution.py:12
  396.7 8.8 %collective-permute-start = (bf16[256,2048]{1,0:T(8,128)(2,1)S(1)}, bf16[256,2048]{1,0:T(8,128)(2,1)}, u32[]{:S(2)}, u32[]{:S(2)}) collective-permute-start(bf16[256,2048]{1,0:T(8,128)(2,1)S(1)} %get-tuple-element.409), channel_id=1, source_target_pairs={{0,16},{16,32},{32,48},{48,64},{64,80},{80,96},{96,112},{112,128},... | collective-permute-start | bytes 3145736 | tf_op jit(solution)/shard_map/while/body/eval_jaxpr/ppermute | solution.py:12
  405.8 19.2 %collective-permute-done = bf16[256,2048]{1,0:T(8,128)(2,1)} collective-permute-done((bf16[256,2048]{1,0:T(8,128)(2,1)S(1)}, bf16[256,2048]{1,0:T(8,128)(2,1)}, u32[]{:S(2)}, u32[]{:S(2)}) %collective-permute-start) | collective-permute-done | bytes 1048608 | tf_op jit(solution)/shard_map/while/body/eval_jaxpr/ppermute | solution.py:12
  430.4 12.4 %collective-permute-done = bf16[256,2048]{1,0:T(8,128)(2,1)} collective-permute-done((bf16[256,2048]{1,0:T(8,128)(2,1)S(1)}, bf16[256,2048]{1,0:T(8,128)(2,1)}, u32[]{:S(2)}, u32[]{:S(2)}) %collective-permute-start) | collective-permute-done | bytes 1048608 | tf_op jit(solution)/shard_map/while/body/eval_jaxpr/ppermute | solution.py:12
  449.4 128.7 %reduce-scatter.2.cloned.1.call-done = bf16[64,1024]{1,0:T(8,128)(2,1)} async-done(((bf16[1024,1024]{1,0:T(8,128)(2,1)}), bf16[64,1024]{1,0:T(8,128)(2,1)}) %reduce-scatter.2.cloned.1.call-update) | async-done | bytes 131088 | tf_op jit(solution)/shard_map/reduce_scatter | solution.py:79
  580.9 7.6 %all-to-all-start = ((bf16[16,2,2048]{2,1,0:T(2,128)(2,1)}), bf16[16,2,2048]{2,1,0:T(2,128)(2,1)S(1)}, u32[]{:S(2)}, u32[]{:S(2)}) async-start(bf16[16,2,2048]{2,1,0:T(2,128)(2,1)} %reshape.73), calls=%async_computation.1 | async-start | bytes 262144 | tf_op jit(solution)/shard_map/all_to_all | solution.py:82
  588.5 8.1 %all-to-all-done = bf16[16,2,2048]{2,1,0:T(2,128)(2,1)S(1)} async-done(((bf16[16,2,2048]{2,1,0:T(2,128)(2,1)}), bf16[16,2,2048]{2,1,0:T(2,128)(2,1)S(1)}, u32[]{:S(2)}, u32[]{:S(2)}) %all-to-all-start) | async-done | bytes 131104 | tf_op jit(solution)/shard_map/all_to_all | solution.py:82
  (153 shorter events, 125.7 us)
Async XLA Ops:
  6.5 571.6 %reduce-scatter.2.cloned.1.call-start = ((), (), s32[]{:S(2)}) async-start(), calls=%async_computation.2 | async-start | bytes 2228224 | tf_op jit(solution)/shard_map/reduce_scatter | solution.py:79
  7.9 4.8 copy-start.1
  12.7 1.0 copy-start.3
  12.7 2.6 copy-start.5
  18.4 2.4 copy-start.2
  20.8 25.0 %copy-start.4 = (bf16[1,256,2048]{2,1,0:T(8,128)(2,1)S(1)}, bf16[1,256,2048]{2,1,0:T(8,128)(2,1)}, u32[]{:S(2)}) copy-start(bf16[1,256,2048]{2,1,0:T(8,128)(2,1)} %pad_maximum_fusion) | copy-start | bytes 3145732
  45.9 27.8 %collective-permute-start = (bf16[256,2048]{1,0:T(8,128)(2,1)S(1)}, bf16[256,2048]{1,0:T(8,128)(2,1)}, u32[]{:S(2)}, u32[]{:S(2)}) collective-permute-start(bf16[256,2048]{1,0:T(8,128)(2,1)S(1)} %get-tuple-element.409), channel_id=1, source_target_pairs={{0,16},{16,32},{32,48},{48,64},{64,80},{80,96},{96,112},{112,128},... | collective-permute-start | bytes 3145736 | tf_op jit(solution)/shard_map/while/body/eval_jaxpr/ppermute | solution.py:12
  73.8 31.1 %collective-permute-start = (bf16[256,2048]{1,0:T(8,128)(2,1)S(1)}, bf16[256,2048]{1,0:T(8,128)(2,1)}, u32[]{:S(2)}, u32[]{:S(2)}) collective-permute-start(bf16[256,2048]{1,0:T(8,128)(2,1)S(1)} %get-tuple-element.409), channel_id=1, source_target_pairs={{0,16},{16,32},{32,48},{48,64},{64,80},{80,96},{96,112},{112,128},... | collective-permute-start | bytes 3145736 | tf_op jit(solution)/shard_map/while/body/eval_jaxpr/ppermute | solution.py:12
  111.0 24.1 %collective-permute-start = (bf16[256,2048]{1,0:T(8,128)(2,1)S(1)}, bf16[256,2048]{1,0:T(8,128)(2,1)}, u32[]{:S(2)}, u32[]{:S(2)}) collective-permute-start(bf16[256,2048]{1,0:T(8,128)(2,1)S(1)} %get-tuple-element.409), channel_id=1, source_target_pairs={{0,16},{16,32},{32,48},{48,64},{64,80},{80,96},{96,112},{112,128},... | collective-permute-start | bytes 3145736 | tf_op jit(solution)/shard_map/while/body/eval_jaxpr/ppermute | solution.py:12
  135.2 25.9 %collective-permute-start = (bf16[256,2048]{1,0:T(8,128)(2,1)S(1)}, bf16[256,2048]{1,0:T(8,128)(2,1)}, u32[]{:S(2)}, u32[]{:S(2)}) collective-permute-start(bf16[256,2048]{1,0:T(8,128)(2,1)S(1)} %get-tuple-element.409), channel_id=1, source_target_pairs={{0,16},{16,32},{32,48},{48,64},{64,80},{80,96},{96,112},{112,128},... | collective-permute-start | bytes 3145736 | tf_op jit(solution)/shard_map/while/body/eval_jaxpr/ppermute | solution.py:12
  161.3 23.0 %collective-permute-start = (bf16[256,2048]{1,0:T(8,128)(2,1)S(1)}, bf16[256,2048]{1,0:T(8,128)(2,1)}, u32[]{:S(2)}, u32[]{:S(2)}) collective-permute-start(bf16[256,2048]{1,0:T(8,128)(2,1)S(1)} %get-tuple-element.409), channel_id=1, source_target_pairs={{0,16},{16,32},{32,48},{48,64},{64,80},{80,96},{96,112},{112,128},... | collective-permute-start | bytes 3145736 | tf_op jit(solution)/shard_map/while/body/eval_jaxpr/ppermute | solution.py:12
  184.4 25.1 %collective-permute-start = (bf16[256,2048]{1,0:T(8,128)(2,1)S(1)}, bf16[256,2048]{1,0:T(8,128)(2,1)}, u32[]{:S(2)}, u32[]{:S(2)}) collective-permute-start(bf16[256,2048]{1,0:T(8,128)(2,1)S(1)} %get-tuple-element.409), channel_id=1, source_target_pairs={{0,16},{16,32},{32,48},{48,64},{64,80},{80,96},{96,112},{112,128},... | collective-permute-start | bytes 3145736 | tf_op jit(solution)/shard_map/while/body/eval_jaxpr/ppermute | solution.py:12
  209.7 23.5 %collective-permute-start = (bf16[256,2048]{1,0:T(8,128)(2,1)S(1)}, bf16[256,2048]{1,0:T(8,128)(2,1)}, u32[]{:S(2)}, u32[]{:S(2)}) collective-permute-start(bf16[256,2048]{1,0:T(8,128)(2,1)S(1)} %get-tuple-element.409), channel_id=1, source_target_pairs={{0,16},{16,32},{32,48},{48,64},{64,80},{80,96},{96,112},{112,128},... | collective-permute-start | bytes 3145736 | tf_op jit(solution)/shard_map/while/body/eval_jaxpr/ppermute | solution.py:12
  233.3 21.2 %collective-permute-start = (bf16[256,2048]{1,0:T(8,128)(2,1)S(1)}, bf16[256,2048]{1,0:T(8,128)(2,1)}, u32[]{:S(2)}, u32[]{:S(2)}) collective-permute-start(bf16[256,2048]{1,0:T(8,128)(2,1)S(1)} %get-tuple-element.409), channel_id=1, source_target_pairs={{0,16},{16,32},{32,48},{48,64},{64,80},{80,96},{96,112},{112,128},... | collective-permute-start | bytes 3145736 | tf_op jit(solution)/shard_map/while/body/eval_jaxpr/ppermute | solution.py:12
  254.6 23.5 %collective-permute-start = (bf16[256,2048]{1,0:T(8,128)(2,1)S(1)}, bf16[256,2048]{1,0:T(8,128)(2,1)}, u32[]{:S(2)}, u32[]{:S(2)}) collective-permute-start(bf16[256,2048]{1,0:T(8,128)(2,1)S(1)} %get-tuple-element.409), channel_id=1, source_target_pairs={{0,16},{16,32},{32,48},{48,64},{64,80},{80,96},{96,112},{112,128},... | collective-permute-start | bytes 3145736 | tf_op jit(solution)/shard_map/while/body/eval_jaxpr/ppermute | solution.py:12
  278.2 24.5 %collective-permute-start = (bf16[256,2048]{1,0:T(8,128)(2,1)S(1)}, bf16[256,2048]{1,0:T(8,128)(2,1)}, u32[]{:S(2)}, u32[]{:S(2)}) collective-permute-start(bf16[256,2048]{1,0:T(8,128)(2,1)S(1)} %get-tuple-element.409), channel_id=1, source_target_pairs={{0,16},{16,32},{32,48},{48,64},{64,80},{80,96},{96,112},{112,128},... | collective-permute-start | bytes 3145736 | tf_op jit(solution)/shard_map/while/body/eval_jaxpr/ppermute | solution.py:12
  302.9 22.2 %collective-permute-start = (bf16[256,2048]{1,0:T(8,128)(2,1)S(1)}, bf16[256,2048]{1,0:T(8,128)(2,1)}, u32[]{:S(2)}, u32[]{:S(2)}) collective-permute-start(bf16[256,2048]{1,0:T(8,128)(2,1)S(1)} %get-tuple-element.409), channel_id=1, source_target_pairs={{0,16},{16,32},{32,48},{48,64},{64,80},{80,96},{96,112},{112,128},... | collective-permute-start | bytes 3145736 | tf_op jit(solution)/shard_map/while/body/eval_jaxpr/ppermute | solution.py:12
  325.2 22.9 %collective-permute-start = (bf16[256,2048]{1,0:T(8,128)(2,1)S(1)}, bf16[256,2048]{1,0:T(8,128)(2,1)}, u32[]{:S(2)}, u32[]{:S(2)}) collective-permute-start(bf16[256,2048]{1,0:T(8,128)(2,1)S(1)} %get-tuple-element.409), channel_id=1, source_target_pairs={{0,16},{16,32},{32,48},{48,64},{64,80},{80,96},{96,112},{112,128},... | collective-permute-start | bytes 3145736 | tf_op jit(solution)/shard_map/while/body/eval_jaxpr/ppermute | solution.py:12
  348.2 23.1 %collective-permute-start = (bf16[256,2048]{1,0:T(8,128)(2,1)S(1)}, bf16[256,2048]{1,0:T(8,128)(2,1)}, u32[]{:S(2)}, u32[]{:S(2)}) collective-permute-start(bf16[256,2048]{1,0:T(8,128)(2,1)S(1)} %get-tuple-element.409), channel_id=1, source_target_pairs={{0,16},{16,32},{32,48},{48,64},{64,80},{80,96},{96,112},{112,128},... | collective-permute-start | bytes 3145736 | tf_op jit(solution)/shard_map/while/body/eval_jaxpr/ppermute | solution.py:12
  371.5 25.1 %collective-permute-start = (bf16[256,2048]{1,0:T(8,128)(2,1)S(1)}, bf16[256,2048]{1,0:T(8,128)(2,1)}, u32[]{:S(2)}, u32[]{:S(2)}) collective-permute-start(bf16[256,2048]{1,0:T(8,128)(2,1)S(1)} %get-tuple-element.409), channel_id=1, source_target_pairs={{0,16},{16,32},{32,48},{48,64},{64,80},{80,96},{96,112},{112,128},... | collective-permute-start | bytes 3145736 | tf_op jit(solution)/shard_map/while/body/eval_jaxpr/ppermute | solution.py:12
  396.7 28.3 %collective-permute-start = (bf16[256,2048]{1,0:T(8,128)(2,1)S(1)}, bf16[256,2048]{1,0:T(8,128)(2,1)}, u32[]{:S(2)}, u32[]{:S(2)}) collective-permute-start(bf16[256,2048]{1,0:T(8,128)(2,1)S(1)} %get-tuple-element.409), channel_id=1, source_target_pairs={{0,16},{16,32},{32,48},{48,64},{64,80},{80,96},{96,112},{112,128},... | collective-permute-start | bytes 3145736 | tf_op jit(solution)/shard_map/while/body/eval_jaxpr/ppermute | solution.py:12
  425.1 17.7 %collective-permute-start = (bf16[256,2048]{1,0:T(8,128)(2,1)S(1)}, bf16[256,2048]{1,0:T(8,128)(2,1)}, u32[]{:S(2)}, u32[]{:S(2)}) collective-permute-start(bf16[256,2048]{1,0:T(8,128)(2,1)S(1)} %get-tuple-element.409), channel_id=1, source_target_pairs={{0,16},{16,32},{32,48},{48,64},{64,80},{80,96},{96,112},{112,128},... | collective-permute-start | bytes 3145736 | tf_op jit(solution)/shard_map/while/body/eval_jaxpr/ppermute | solution.py:12
  446.3 151.3 %copy-start = (s32[1024,256]{1,0:T(8,128)S(1)}, s32[1024,256]{1,0:T(8,128)}, u32[]{:S(2)}) copy-start(s32[1024,256]{1,0:T(8,128)} %param.17) | copy-start | bytes 3145732
  580.9 15.7 %all-to-all-start = ((bf16[16,2,2048]{2,1,0:T(2,128)(2,1)}), bf16[16,2,2048]{2,1,0:T(2,128)(2,1)S(1)}, u32[]{:S(2)}, u32[]{:S(2)}) async-start(bf16[16,2,2048]{2,1,0:T(2,128)(2,1)} %reshape.73), calls=%async_computation.1 | async-start | bytes 262144 | tf_op jit(solution)/shard_map/all_to_all | solution.py:82
Sparse Core Ops, SparseCore 0:
  449.5 128.5 reduce-scatter.1
where the time goes:
time: 614 us; the launch traced here: 612 us
  waiting for transfers between devices  431 us (70%)
  starting transfers between devices  98.3 us (16%)
  other arithmetic  35.7 us (6%)
  local copies, waits for them, and re-layouts  19.1 us (3%)
  between operations  14.3 us (2%)
  matrix products  13 us (2%)
    ppermute x16, waiting for transfers between devices, from_behind(): lax.ppermute(value, axis, [(source, source + steps) for source in range(l...  294 us
    reduce_scatter x1, waiting for transfers between devices, shards(): lax.psum_scatter((partial_value * factor).astype(jnp.bfloat16), 'freq', s...  129 us
    ppermute x16, starting transfers between devices, from_behind(): lax.ppermute(value, axis, [(source, source + steps) for source in range(l...  90.7 us
    concatenate x1, other arithmetic, make_block(): return jnp.concatenate([upper, lower], axis=0)  23.7 us
  transfers between devices with their start and end apart: 18, of which 18 were waited for; matrix products, arithmetic and copies ran while one was open for 1% of the time, Pallas kernels for 0%

commit v1 on v0

v1 whole, which is shorter than its diff:
```python
import math

import jax
import jax.numpy as jnp
from jax import lax
from jax.experimental import pallas as pl
from jax.experimental.pallas import tpu as pltpu
from jax.sharding import PartitionSpec as P

MESH = pl.DeviceIdType.MESH
BATCH = 8


def chain_kernel(depth_count, batch_count, e_ref, x_ref, out_ref, inbuf, send_sem, recv_sem):
    d = lax.axis_index("depth")
    barrier = pltpu.get_barrier_semaphore()

    @pl.when(d > 0)
    def _():
        pl.semaphore_signal(barrier, inc=1, device_id={"depth": d - 1}, device_id_type=MESH)

    @pl.when(d < depth_count - 1)
    def _():
        pl.semaphore_wait(barrier, 1)

    @pl.when(d == 0)
    def _():
        inbuf[...] = x_ref[...]

    half = 2 * BATCH

    def hop(b):
        rows = pl.ds(pl.multiple_of(b * half, half), half)
        return pltpu.make_async_remote_copy(
            src_ref=out_ref.at[:, rows, :],
            dst_ref=inbuf.at[:, rows, :],
            send_sem=send_sem.at[b],
            recv_sem=recv_sem.at[b],
            device_id={"depth": d + 1},
            device_id_type=MESH,
        )

    def step(b, carry):
        rows = pl.ds(pl.multiple_of(b * half, half), half)

        @pl.when(d > 0)
        def _():
            hop(b).wait_recv()

        values = inbuf[:, rows, :].reshape(2 * half, -1)
        first = jnp.dot(values, e_ref[0], preferred_element_type=jnp.float32)
        second = jnp.dot(values, e_ref[1], preferred_element_type=jnp.float32)
        m = BATCH
        source = jnp.concatenate(
            [first[:m] - second[m : 2 * m], second[:m] + first[m : 2 * m]], axis=0
        )
        record = jnp.concatenate(
            [first[2 * m : 3 * m] + second[3 * m :], first[3 * m :] - second[2 * m : 3 * m]], axis=0
        )
        out_ref[0, rows, :] = source.astype(jnp.bfloat16)
        out_ref[1, rows, :] = record.astype(jnp.bfloat16)

        @pl.when(d < depth_count - 1)
        def _():
            hop(b).start()

        return carry

    lax.fori_loop(0, batch_count, step, 0)

    @pl.when(d < depth_count - 1)
    def _():
        def drain(b, carry):
            hop(b).wait_send()
            return carry

        lax.fori_loop(0, batch_count, drain, 0)


def run_chain(extrap, packed, depth_count):
    rows = packed.shape[1]
    points = packed.shape[2]
    batch_count = rows // (2 * BATCH)

    def body(*refs):
        chain_kernel(depth_count, batch_count, *refs)

    return pl.pallas_call(
        body,
        out_shape=jax.ShapeDtypeStruct(packed.shape, jnp.bfloat16),
        in_specs=[pl.BlockSpec(memory_space=pltpu.VMEM)] * 2,
        out_specs=pl.BlockSpec(memory_space=pltpu.VMEM),
        scratch_shapes=[
            pltpu.VMEM((2, rows, points), jnp.bfloat16),
            pltpu.SemaphoreType.DMA((batch_count,)),
            pltpu.SemaphoreType.DMA((batch_count,)),
        ],
        compiler_params=pltpu.CompilerParams(
            collective_id=0, has_side_effects=True, vmem_limit_bytes=32 * 1024 * 1024
        ),
        name="chain",
    )(extrap, packed)


def shards(extrap, source_field, record_field, shot_of_record, freq_index, angle_lag):
    depth_count = lax.axis_size("depth")
    freq_count = lax.axis_size("freq")
    points = source_field.shape[3]
    shot_count = source_field.shape[1]
    paired = jnp.take(source_field[0], shot_of_record, axis=0)

    def pack(field):
        split = field.reshape(shot_count // BATCH, BATCH, 2, points)
        return split.transpose(0, 2, 1, 3).reshape(2 * shot_count, points)

    packed = jnp.stack([pack(paired), pack(record_field[0])])
    finished = run_chain(extrap[0, 0], packed, depth_count)
    factor = (
        (freq_index[0].astype(jnp.float32) + 1.0)
        / (8 * freq_count)
        / math.sqrt(shot_count * freq_count)
    )
    partial_value = lax.dot_general(
        finished[0], finished[1], (((0,), (0,)), ((), ())), preferred_element_type=jnp.float32
    )
    image_panel = lax.psum_scatter(
        (partial_value * factor).astype(jnp.bfloat16), "freq", scatter_dimension=0, tiled=True
    )
    gathered = lax.all_to_all(
        image_panel[:, None, :], "depth", split_axis=0, concat_axis=1, tiled=True
    )
    row_count = gathered.shape[0]
    padded = jnp.concatenate([gathered, jnp.zeros_like(gathered)], axis=1)

    def add_lagged(lag_value, stacked_sum):
        shifted = lax.dynamic_slice_in_dim(padded, lag_value, depth_count, 1).reshape(
            row_count * depth_count, points
        )
        selector = (angle_lag == lag_value).astype(jnp.bfloat16)
        return stacked_sum + jnp.dot(shifted, selector, preferred_element_type=jnp.float32)

    stacked_sum = lax.fori_loop(
        0,
        depth_count,
        add_lagged,
        jnp.zeros((row_count * depth_count, angle_lag.shape[1]), jnp.float32),
    )
    return (stacked_sum / math.sqrt(points)).reshape(row_count, depth_count, angle_lag.shape[1])


def solution(mesh):
    placed = (
        P("depth", "freq", None, None, None),
        P("freq", None, None, None),
        P("freq", None, None, None),
        P(),
        P("freq"),
        P(),
    )
    return jax.shard_map(
        shards,
        mesh=mesh,
        in_specs=placed,
        out_specs=P(("freq", "depth"), None, None),
        check_vma=False,
    )
```

time: 614 us -> 218 us (0.36)
  waiting for transfers between devices: 431 us -> 141 us
  starting transfers between devices: 98.3 us -> 7.66 us
  Pallas kernels: 0 us -> 33.8 us
  other arithmetic: 35.7 us -> 4.57 us
  local copies, waits for them, and re-layouts: 19.1 us -> 8.14 us
    ppermute x16 -> x0, waiting for transfers between devices: 294 us -> none  [from_behind(): lax.ppermute(value, axis, [(source, source + steps) for source in range(l...]
    ppermute x16 -> x0, starting transfers between devices: 90.7 us -> none  [from_behind(): lax.ppermute(value, axis, [(source, source + steps) for source in range(l...]
    pallas_call x0 -> x1, Pallas kernels: none -> 33.8 us  [run_chain(): pl.pallas_call(body, out_shape=jax.ShapeDtypeStruct(packed.shape, jnp.bfl...]
    concatenate x2 -> x0, other arithmetic: 25.9 us -> none  [the longest x1 23.7 us: make_block(): return jnp.concatenate([upper, lower], axis=0)]
  transfers between devices with their start and end apart: 18 -> 2, of which waited for: 18 -> 2; matrix products, arithmetic and copies ran while one was open for 1% -> 0% of each run, Pallas kernels for 0% -> 0%
where the time goes in v1:
time: 218 us; the launch traced here: 217 us
  waiting for transfers between devices  141 us (65%)
  Pallas kernels  33.8 us (16%)
  between operations  14.2 us (7%)
  local copies, waits for them, and re-layouts  8.14 us (4%)
  starting transfers between devices  7.66 us (4%)
  matrix products  7.02 us (3%)
  other arithmetic  4.57 us (2%)
    reduce_scatter x1, waiting for transfers between devices, shards(): lax.psum_scatter((partial_value * factor).astype(jnp.bfloat16), 'freq', s...  133 us
    pallas_call x1, Pallas kernels, run_chain(): pl.pallas_call(body, out_shape=jax.ShapeDtypeStruct(packed.shape, jnp.bfl...  33.8 us
    all_to_all x1, waiting for transfers between devices, shards(): lax.all_to_all(image_panel[:, None, :], 'depth', split_axis=0, concat_axi...  8.08 us
    all_to_all x1, starting transfers between devices, shards(): lax.all_to_all(image_panel[:, None, :], 'depth', split_axis=0, concat_axi...  7.66 us
    dot_general x16, matrix products, add_lagged(): jnp.dot(shifted, selector, preferred_element_type=jnp.float32)  4.92 us
  transfers between devices with their start and end apart: 2, of which 2 were waited for; matrix products, arithmetic and copies ran while one was open for 0% of the time, Pallas kernels for 0%

profile of v1, /device:TPU:32, one launch (start us, length us, event | category | flops | bytes accessed | tf_op | source)
XLA Modules:
  0.0 216.7 jit_solution(7630549818406183027)
XLA Ops:
  6.5 0.7 compare_select_fusion
  7.3 0.7 compare_and_fusion
  8.0 1.2 copy.18
  9.9 1.6 gather_fusion
  11.7 2.2 %copy-done.1 = bf16[1,1,2,1024,1024]{4,3,2,1,0:T(8,128)(2,1)S(1)} copy-done((bf16[1,1,2,1024,1024]{4,3,2,1,0:T(8,128)(2,1)S(1)}, bf16[1,1,2,1024,1024]{4,3,2,1,0:T(8,128)(2,1)}, u32[]{:S(2)}) %copy-start.1) | copy-done | bytes 4194328
  13.9 33.8 %chain.1 = bf16[2,256,1024]{2,1,0:T(8,128)(2,1)S(1)} custom-call(bf16[2,1024,1024]{2,1,0:T(8,128)(2,1)S(1)} %bitcast.29, bf16[2,256,1024]{2,1,0:T(8,128)(2,1)S(1)} %pad_maximum_fusion.refs_1_), custom_call_target="tpu_custom_call" | custom-call | tf_op jit(solution)/shard_map/chain/pallas_call | solution.py:88
  47.7 2.1 multiply_convert_fusion
  49.8 132.6 %reduce-scatter.2.cloned.1.call-done = bf16[64,1024]{1,0:T(8,128)(2,1)} async-done(((bf16[1024,1024]{1,0:T(8,128)(2,1)}), bf16[64,1024]{1,0:T(8,128)(2,1)}) %reduce-scatter.2.cloned.1.call-update) | async-done | bytes 131088 | tf_op jit(solution)/shard_map/reduce_scatter | solution.py:126
  182.5 0.5 broadcast.18
  183.0 1.6 reduce.1
  184.6 0.7 reshape.36
  185.3 7.7 %all-to-all-start = ((bf16[16,2,2048]{2,1,0:T(2,128)(2,1)}), bf16[16,2,2048]{2,1,0:T(2,128)(2,1)S(1)}, u32[]{:S(2)}, u32[]{:S(2)}) async-start(bf16[16,2,2048]{2,1,0:T(2,128)(2,1)} %reshape.36), calls=%async_computation.1 | async-start | bytes 262144 | tf_op jit(solution)/shard_map/all_to_all | solution.py:129
  193.0 8.1 %all-to-all-done = bf16[16,2,2048]{2,1,0:T(2,128)(2,1)S(1)} async-done(((bf16[16,2,2048]{2,1,0:T(2,128)(2,1)}), bf16[16,2,2048]{2,1,0:T(2,128)(2,1)S(1)}, u32[]{:S(2)}, u32[]{:S(2)}) %all-to-all-start) | async-done | bytes 131104 | tf_op jit(solution)/shard_map/all_to_all | solution.py:129
  201.2 0.7 reduce
  202.1 7.2 %while.14 = (s32[]{:T(128)}, f32[64,256]{1,0:T(8,128)S(1)}, bf16[4,32,1024]{2,0,1:T(4,128)(2,1)S(1)}, s32[1024,256]{1,0:T(8,128)S(1)}, s32[]{:T(128)}, /*index=5*/s32[]{:T(128)}) while((s32[]{:T(128)}, f32[64,256]{1,0:T(8,128)S(1)}, bf16[4,32,1024]{2,0,1:T(4,128)(2,1)S(1)}, s32[1024,256]{1,0:T(8,128)S(1)}, s32[]{:T(128)}, ...), condition=%wide.region_2.3_spmd.clone, body=%wide.region_1.2_spmd.clone.sunk | while | flops 33849344 | bytes 1835095 | solution.py:142
  202.7 0.3 convolution_add_fusion.2
  203.1 0.3 convolution_add_fusion.2
  204.5 0.3 convolution_add_fusion.2
  204.9 0.3 convolution_add_fusion.2
  205.4 0.3 convolution_add_fusion.2
  205.8 0.3 convolution_add_fusion.2
  208.5 0.3 convolution_add_fusion.2
  208.9 0.3 convolution_add_fusion.2
  209.2 0.6 broadcast_multiply_fusion
  (55 shorter events, 4.6 us)
Async XLA Ops:
  6.5 3.3 %copy-start = (bf16[1,128,2,1024]{3,2,1,0:T(2,128)(2,1)S(1)}, bf16[1,128,2,1024]{3,2,1,0:T(2,128)(2,1)}, u32[]{:S(2)}) copy-start(bf16[1,128,2,1024]{3,2,1,0:T(2,128)(2,1)} %param.9) | copy-start | bytes 1572868
  6.5 175.9 %reduce-scatter.2.cloned.1.call-start = ((), (), s32[]{:S(2)}) async-start(), calls=%async_computation.2 | async-start | bytes 2228224 | tf_op jit(solution)/shard_map/reduce_scatter | solution.py:126
  11.7 2.2 %copy-start.1 = (bf16[1,1,2,1024,1024]{4,3,2,1,0:T(8,128)(2,1)S(1)}, bf16[1,1,2,1024,1024]{4,3,2,1,0:T(8,128)(2,1)}, u32[]{:S(2)}) copy-start(bf16[1,1,2,1024,1024]{4,3,2,1,0:T(8,128)(2,1)} %param.8) | copy-start | bytes 12582916
  47.7 154.4 %copy-start.2 = (s32[1024,256]{1,0:T(8,128)S(1)}, s32[1024,256]{1,0:T(8,128)}, u32[]{:S(2)}) copy-start(s32[1024,256]{1,0:T(8,128)} %param.13) | copy-start | bytes 3145732
  185.3 15.7 %all-to-all-start = ((bf16[16,2,2048]{2,1,0:T(2,128)(2,1)}), bf16[16,2,2048]{2,1,0:T(2,128)(2,1)S(1)}, u32[]{:S(2)}, u32[]{:S(2)}) async-start(bf16[16,2,2048]{2,1,0:T(2,128)(2,1)} %reshape.36), calls=%async_computation.1 | async-start | bytes 262144 | tf_op jit(solution)/shard_map/all_to_all | solution.py:129
Sparse Core Ops, SparseCore 0:
  50.0 132.4 reduce-scatter.1

commit v2 on v1

v2 whole, which is shorter than its diff:
```python
import math

import jax
import jax.numpy as jnp
from jax import lax
from jax.experimental import pallas as pl
from jax.experimental.pallas import tpu as pltpu
from jax.sharding import PartitionSpec as P

MESH = pl.DeviceIdType.MESH
BATCH = 8
DEPTHS = 16
ROWS = 64
POINTS = 1024
ANGLES = 256
SHOTS = 128
LANES = 128
BATCHES = SHOTS // BATCH
HALF = 2 * BATCH
PIECE = ROWS // DEPTHS
ORDER = [(1, 2), (1, 1), (1, 3), (1, 0), (0, 2), (0, 1), (0, 3), (0, 0)]
F32 = jnp.float32
BF16 = jnp.bfloat16


def kernel(
    e_hbm, x_ref, factor_ref, lag_ref, out_ref,
    e_ref, inbuf, fin, sel, part, corein, two, one, three, rel_up, rel_down, from_down, from_up,
    ysend, yin, acc, pieces, gath, xs, g,
    e_sem, chain_send, chain_recv, core_send, core_recv, x_send, x_recv, y_send, y_recv, d_send, d_recv,
):
    d = lax.axis_index("depth")
    f = lax.axis_index("freq")
    core = f % 2
    x = (f // 2) % 4
    yh = f // 8
    partner = f + 1 - 2 * core
    up = yh * 8 + ((x + 1) % 4) * 2 + core
    down = yh * 8 + ((x + 3) % 4) * 2 + core
    across = f + 8 - 16 * yh

    load_e = pltpu.make_async_copy(e_hbm, e_ref, e_sem)
    load_e.start()
    barrier = pltpu.get_barrier_semaphore()
    for other in (partner, up, down, across):
        pl.semaphore_signal(barrier, inc=1, device_id={"freq": other}, device_id_type=MESH)

    def greet(k, carry):
        pl.semaphore_signal(
            barrier, inc=1, device_id={"depth": (d + k) % DEPTHS}, device_id_type=MESH
        )
        return carry

    lax.fori_loop(1, DEPTHS, greet, 0)

    def build():
        def one_lag(lag, carry):
            sel[lag] = jnp.where(lag_ref[...] == lag, 1.0, 0.0).astype(BF16)
            g[lag, :, ROWS:, :] = jnp.zeros((2, ROWS, LANES), F32)
            return carry

        lax.fori_loop(0, DEPTHS, one_lag, 0)

    @pl.when(d > 0)
    def _():
        build()

    @pl.when(d == 0)
    def _():
        inbuf[...] = x_ref[...]

    load_e.wait()
    pl.semaphore_wait(barrier, 4 + DEPTHS - 1)

    def hop(b):
        rows = pl.ds(pl.multiple_of(b * HALF, HALF), HALF)
        return pltpu.make_async_remote_copy(
            src_ref=fin.at[:, rows, :],
            dst_ref=inbuf.at[:, rows, :],
            send_sem=chain_send.at[b],
            recv_sem=chain_recv.at[b],
            device_id={"depth": d + 1},
            device_id_type=MESH,
        )

    def step(b, carry):
        rows = pl.ds(pl.multiple_of(b * HALF, HALF), HALF)

        @pl.when(d > 0)
        def _():
            hop(b).wait_recv()

        values = inbuf[:, rows, :].reshape(2 * HALF, POINTS)
        first = jnp.dot(values, e_ref[0], preferred_element_type=F32)
        second = jnp.dot(values, e_ref[1], preferred_element_type=F32)
        m = BATCH
        source = jnp.concatenate(
            [first[:m] - second[m : 2 * m], second[:m] + first[m : 2 * m]], axis=0
        )
        record = jnp.concatenate(
            [first[2 * m : 3 * m] + second[3 * m :], first[3 * m :] - second[2 * m : 3 * m]], axis=0
        )
        fin[0, rows, :] = source.astype(BF16)
        fin[1, rows, :] = record.astype(BF16)

        @pl.when(d < DEPTHS - 1)
        def _():
            hop(b).start()

        return carry

    lax.fori_loop(0, BATCHES, step, 0)

    mine = pl.ds(pl.multiple_of(core * ROWS, ROWS), ROWS)
    theirs = pl.ds(pl.multiple_of((1 - core) * ROWS, ROWS), ROWS)

    def to_core(t):
        return pltpu.make_async_remote_copy(
            src_ref=part.at[t, theirs, :],
            dst_ref=corein.at[t],
            send_sem=core_send.at[t],
            recv_sem=core_recv.at[t],
            device_id={"freq": partner},
            device_id_type=MESH,
        )

    factor = factor_ref[0]
    for t, (q, r) in enumerate(ORDER):
        block = (yh + q * (1 - 2 * yh)) * 4 + (x + r) % 4
        columns = pl.ds(pl.multiple_of(block * 2 * ROWS, 2 * ROWS), 2 * ROWS)
        term = lax.dot_general(
            fin[0, :, columns], fin[1], (((0,), (0,)), ((), ())), preferred_element_type=F32
        )
        part[t] = (term * factor).astype(BF16)
        to_core(t).start()

    @pl.when(d == 0)
    def _():
        build()

    def pair(t, rows=slice(0, ROWS)):
        own = part[t, mine, :][rows]
        return own.astype(F32) + corein[t, rows, :].astype(F32)

    def ring(src, dst, s, target):
        return pltpu.make_async_remote_copy(
            src_ref=src,
            dst_ref=dst,
            send_sem=x_send.at[s],
            recv_sem=x_recv.at[s],
            device_id={"freq": target},
            device_id_type=MESH,
        )

    low, high = slice(0, ROWS // 2), slice(ROWS // 2, ROWS)
    copies = {}
    for q in (0, 1):
        base = 6 * q
        lo, hi = pl.ds(0, ROWS // 2), pl.ds(ROWS // 2, ROWS // 2)
        copies[q] = dict(
            two_up=ring(two.at[q, lo, :], rel_up.at[q], base, up),
            two_down=ring(two.at[q, hi, :], rel_down.at[q], base + 1, down),
            one_now=ring(one.at[q, hi, :], from_down.at[q, hi, :], base + 2, up),
            one_late=ring(one.at[q, lo, :], from_down.at[q, lo, :], base + 3, up),
            three_now=ring(three.at[q, lo, :], from_up.at[q, lo, :], base + 4, down),
            three_late=ring(three.at[q, hi, :], from_up.at[q, hi, :], base + 5, down),
        )

    def far(q):
        t = ORDER.index((q, 2))
        to_core(t).wait_recv()
        two[q] = pair(t).astype(BF16)
        copies[q]["two_up"].start()
        copies[q]["two_down"].start()

    def near(q):
        t = ORDER.index((q, 1))
        to_core(t).wait_recv()
        one[q] = pair(t).astype(BF16)
        copies[q]["one_now"].start()
        t = ORDER.index((q, 3))
        to_core(t).wait_recv()
        three[q] = pair(t).astype(BF16)
        copies[q]["three_now"].start()

    def relay(q):
        copies[q]["two_up"].wait_recv()
        one[q, low, :] = (one[q, low, :].astype(F32) + rel_up[q].astype(F32)).astype(BF16)
        copies[q]["one_late"].start()
        copies[q]["two_down"].wait_recv()
        three[q, high, :] = (three[q, high, :].astype(F32) + rel_down[q].astype(F32)).astype(BF16)
        copies[q]["three_late"].start()

    def collect(q):
        t = ORDER.index((q, 0))
        to_core(t).wait_recv()
        for name in ("one_now", "three_now", "one_late", "three_late"):
            copies[q][name].wait_recv()
        return pair(t) + from_down[q].astype(F32) + from_up[q].astype(F32)

    over = pltpu.make_async_remote_copy(
        src_ref=ysend, dst_ref=yin, send_sem=y_send, recv_sem=y_recv,
        device_id={"freq": across}, device_id_type=MESH,
    )
    far(1)
    near(1)
    far(0)
    relay(1)
    near(0)
    ysend[...] = collect(1).astype(BF16)
    over.start()
    relay(0)
    acc[...] = collect(0)
    over.wait_recv()
    acc[...] = acc[...] + yin[...].astype(F32)
    for k in range(DEPTHS):
        pieces[k] = acc[PIECE * k : PIECE * (k + 1), :].astype(BF16)

    def deal(k):
        target = (d + k) % DEPTHS
        return pltpu.make_async_remote_copy(
            src_ref=pieces.at[target],
            dst_ref=gath.at[d],
            send_sem=d_send.at[k],
            recv_sem=d_recv.at[k],
            device_id={"depth": target},
            device_id_type=MESH,
        )

    def arrival(k):
        source = (d + DEPTHS - k) % DEPTHS
        return pltpu.make_async_remote_copy(
            src_ref=pieces.at[source],
            dst_ref=gath.at[source],
            send_sem=d_send.at[k],
            recv_sem=d_recv.at[k],
            device_id={"depth": source},
            device_id_type=MESH,
        )

    def send_piece(k, carry):
        deal(k).start()
        return carry

    lax.fori_loop(1, DEPTHS, send_piece, 0)
    gath[d] = pieces[d]

    def take_piece(k, carry):
        arrival(k).wait_recv()
        return carry

    lax.fori_loop(1, DEPTHS, take_piece, 0)
    for k in range(DEPTHS):
        xs[PIECE * k : PIECE * (k + 1), :] = gath[k].astype(F32)

    def stack(lag, carry):
        term = jnp.dot(xs[...].astype(BF16), sel[lag], preferred_element_type=F32)
        g[lag, 0, 0:ROWS, :] = term[:, :LANES]
        g[lag, 1, 0:ROWS, :] = term[:, LANES:]
        return carry

    lax.fori_loop(0, DEPTHS, stack, 0)
    scale = 1.0 / math.sqrt(POINTS)
    for row in range(PIECE):
        for side in range(2):
            total = g[0, side, pl.ds(row, DEPTHS, stride=PIECE), :]
            for lag in range(1, DEPTHS):
                total = total + g[lag, side, pl.ds(PIECE * lag + row, DEPTHS, stride=PIECE), :]
            out_ref[row, :, LANES * side : LANES * (side + 1)] = total * scale

    @pl.when(d < DEPTHS - 1)
    def _():
        def drain(b, carry):
            hop(b).wait_send()
            return carry

        lax.fori_loop(0, BATCHES, drain, 0)

    for t in range(len(ORDER)):
        to_core(t).wait_send()
    for q in (0, 1):
        for copy in copies[q].values():
            copy.wait_send()
    over.wait_send()

    def drain_piece(k, carry):
        deal(k).wait_send()
        return carry

    lax.fori_loop(1, DEPTHS, drain_piece, 0)


def migrate(extrap, packed, factor, angle_lag):
    vmem = pl.BlockSpec(memory_space=pltpu.VMEM)
    return pl.pallas_call(
        kernel,
        out_shape=jax.ShapeDtypeStruct((PIECE, DEPTHS, ANGLES), F32),
        in_specs=[
            pl.BlockSpec(memory_space=pl.ANY),
            vmem,
            pl.BlockSpec(memory_space=pltpu.SMEM),
            vmem,
        ],
        out_specs=vmem,
        scratch_shapes=[
            pltpu.VMEM((2, POINTS, POINTS), BF16),
            pltpu.VMEM((2, 2 * SHOTS, POINTS), BF16),
            pltpu.VMEM((2, 2 * SHOTS, POINTS), BF16),
            pltpu.VMEM((DEPTHS, POINTS, ANGLES), BF16),
            pltpu.VMEM((8, 2 * ROWS, POINTS), BF16),
            pltpu.VMEM((8, ROWS, POINTS), BF16),
            pltpu.VMEM((2, ROWS, POINTS), BF16),
            pltpu.VMEM((2, ROWS, POINTS), BF16),
            pltpu.VMEM((2, ROWS, POINTS), BF16),
            pltpu.VMEM((2, ROWS // 2, POINTS), BF16),
            pltpu.VMEM((2, ROWS // 2, POINTS), BF16),
            pltpu.VMEM((2, ROWS, POINTS), BF16),
            pltpu.VMEM((2, ROWS, POINTS), BF16),
            pltpu.VMEM((ROWS, POINTS), BF16),
            pltpu.VMEM((ROWS, POINTS), BF16),
            pltpu.VMEM((ROWS, POINTS), F32),
            pltpu.VMEM((DEPTHS, PIECE, POINTS), BF16),
            pltpu.VMEM((DEPTHS, PIECE, POINTS), BF16),
            pltpu.VMEM((ROWS, POINTS), F32),
            pltpu.VMEM((DEPTHS, 2, 2 * ROWS, LANES), F32),
            pltpu.SemaphoreType.DMA,
            pltpu.SemaphoreType.DMA((BATCHES,)),
            pltpu.SemaphoreType.DMA((BATCHES,)),
            pltpu.SemaphoreType.DMA((8,)),
            pltpu.SemaphoreType.DMA((8,)),
            pltpu.SemaphoreType.DMA((12,)),
            pltpu.SemaphoreType.DMA((12,)),
            pltpu.SemaphoreType.DMA,
            pltpu.SemaphoreType.DMA,
            pltpu.SemaphoreType.DMA((DEPTHS,)),
            pltpu.SemaphoreType.DMA((DEPTHS,)),
        ],
        compiler_params=pltpu.CompilerParams(
            collective_id=0, has_side_effects=True, vmem_limit_bytes=48 * 1024 * 1024
        ),
        name="migrate",
    )(extrap, packed, factor, angle_lag)


def shards(extrap, source_field, record_field, shot_of_record, freq_index, angle_lag):
    freq_count = lax.axis_size("freq")
    paired = source_field[0].at[shot_of_record].get(mode="promise_in_bounds")

    def pack(field):
        split = field.reshape(BATCHES, BATCH, 2, POINTS)
        return split.transpose(0, 2, 1, 3).reshape(2 * SHOTS, POINTS)

    packed = jnp.stack([pack(paired), pack(record_field[0])])
    factor = (
        (freq_index.astype(F32) + 1.0) / (8 * freq_count) / math.sqrt(SHOTS * freq_count)
    )
    return migrate(extrap[0, 0], packed, factor, angle_lag)


def solution(mesh):
    placed = (
        P("depth", "freq", None, None, None),
        P("freq", None, None, None),
        P("freq", None, None, None),
        P(),
        P("freq"),
        P(),
    )
    return jax.shard_map(
        shards,
        mesh=mesh,
        in_specs=placed,
        out_specs=P(("freq", "depth"), None, None),
        check_vma=False,
    )
```

time: 218 us -> 129 us (0.59)
  waiting for transfers between devices: 141 us -> 0 us
  Pallas kernels: 33.8 us -> 124 us
  between operations: 14.2 us -> 0.69 us
  starting transfers between devices: 7.66 us -> 0 us
  matrix products: 7.02 us -> 0 us
  local copies, waits for them, and re-layouts: 8.14 us -> 3.8 us
  other arithmetic: 4.57 us -> 0.88 us
    reduce_scatter x1 -> x0, waiting for transfers between devices: 133 us -> none  [shards(): lax.psum_scatter((partial_value * factor).astype(jnp.bfloat16), 'freq', s...]
    pallas_call x1, Pallas kernels: 33.8 us -> 124 us  [migrate(): pl.pallas_call(kernel, out_shape=jax.ShapeDtypeStruct((PIECE, DEPTHS, ANG...]
    all_to_all x1 -> x0, waiting for transfers between devices: 8.08 us -> none  [shards(): lax.all_to_all(image_panel[:, None, :], 'depth', split_axis=0, concat_axi...]
    all_to_all x1 -> x0, starting transfers between devices: 7.66 us -> none  [shards(): lax.all_to_all(image_panel[:, None, :], 'depth', split_axis=0, concat_axi...]
    dot_general x17 -> x0, matrix products: 7.02 us -> none  [the longest x16 4.92 us: add_lagged(): jnp.dot(shifted, selector, preferred_element_type=jnp.float32)]
  transfers between devices with their start and end apart: 2 -> 0, of which waited for: 2 -> 0; matrix products, arithmetic and copies ran while one was open for 0% -> 0% of each run, Pallas kernels for 0% -> 0%
where the time goes in v2:
time: 129 us
  Pallas kernels  124 us (96%)
  local copies, waits for them, and re-layouts  3.8 us (3%)
    pallas_call x1, Pallas kernels, migrate(): pl.pallas_call(kernel, out_shape=jax.ShapeDtypeStruct((PIECE, DEPTHS, ANG...  124 us

profile of v2, /device:TPU:32, one launch (start us, length us, event | category | flops | bytes accessed | tf_op | source)
XLA Modules:
  0.0 129.3 jit_solution(5160457599832437799)
XLA Ops:
  0.0 0.0 copy-start
  0.0 0.0 copy-start.1
  0.0 0.8 compare_select_fusion
  0.8 0.3 copy-done
  1.1 1.6 %gather_fusion = bf16[128,2,1024]{2,1,0:T(2,128)(2,1)S(1)} fusion(bf16[128,2,1024]{2,1,0:T(2,128)(2,1)S(1)} %bitcast.10, s32[1024]{0:T(1024)S(1)} %pad_clamp_fusion), kind=kCustom, calls=%fused_computation | custom fusion | bytes 1049088 | tf_op jit(solution)/shard_map/gather | solution.py:347
  2.7 0.1 copy.7
  2.8 1.2 copy.8
  4.0 0.1 pad_maximum_fusion.x_ref
  4.7 0.0 copy-done.1
  4.7 123.9 %migrate.1 = f32[4,16,256]{2,1,0:T(8,128)S(1)} custom-call(bf16[2,1024,1024]{2,1,0:T(8,128)(2,1)} %bitcast.11, bf16[2,256,1024]{2,1,0:T(8,128)(2,1)S(1)} %pad_maximum_fusion.x_ref, f32[1]{0:T(128)S(6)} %div.4.factor_ref, s32[1024,256]{1,0:T(8,128)S(1)} %copy-done.1), custom_call_target="tpu_custom_call" | custom-call | tf_op jit(solution)/shard_map/migrate/pallas_call | solution.py:295
  128.6 0.6 copy.11
  (1 shorter events, 0.0 us)
Async XLA Ops:
  0.0 1.1 copy-start
  0.0 4.7 %copy-start.1 = (s32[1024,256]{1,0:T(8,128)S(1)}, s32[1024,256]{1,0:T(8,128)}, u32[]{:S(2)}) copy-start(s32[1024,256]{1,0:T(8,128)} %lag_ref.1) | copy-start | bytes 3145732

commit v3 on v2

--- a/solution.py
+++ b/solution.py
@@ -8,7 +8,7 @@
 from jax.sharding import PartitionSpec as P
 
 MESH = pl.DeviceIdType.MESH
-BATCH = 8
+BATCH = 4
 DEPTHS = 16
 ROWS = 64
 POINTS = 1024
@@ -23,11 +23,29 @@
 BF16 = jnp.bfloat16
 
 
+def swap_parts(a, b):
+    rolled = jnp.concatenate(
+        [pltpu.roll(b[:HALF], BATCH, 0), pltpu.roll(b[HALF:], BATCH, 0)], axis=0
+    )
+    row = lax.broadcasted_iota(jnp.int32, rolled.shape, 0)
+    minus = (row < BATCH) | (row >= HALF + BATCH)
+    return a + jnp.where(minus, -rolled, rolled)
+
+
+def expand(part):
+    shape = (SHOTS, 2 * SHOTS)
+    shot = lax.broadcasted_iota(jnp.int32, shape, 0)
+    row = lax.broadcasted_iota(jnp.int32, shape, 1)
+    place = row - BATCH * part
+    hit = (place >= 0) & (place % HALF < BATCH) & ((place // HALF) * BATCH + place % HALF == shot)
+    return jnp.where(hit, 1.0, 0.0).astype(BF16)
+
+
 def kernel(
-    e_hbm, x_ref, factor_ref, lag_ref, out_ref,
-    e_ref, inbuf, fin, sel, part, corein, two, one, three, rel_up, rel_down, from_down, from_up,
+    e_hbm, x_ref, shot_ref, factor_ref, lag_ref, out_ref,
+    e_ref, inbuf, fin, field, sel, part, corein, two, one, three, rel_up, rel_down, from_down, from_up,
     ysend, yin, acc, pieces, gath, xs, g,
-    e_sem, chain_send, chain_recv, core_send, core_recv, x_send, x_recv, y_send, y_recv, d_send, d_recv,
+    e_sem, chain_send, chain_recv, core_send, core_recv, x_send, x_recv, y_send, y_recv, d_send, d_recv, greet_sem,
 ):
     d = lax.axis_index("depth")
     f = lax.axis_index("freq")
@@ -45,13 +63,9 @@
     for other in (partner, up, down, across):
         pl.semaphore_signal(barrier, inc=1, device_id={"freq": other}, device_id_type=MESH)
 
-    def greet(k, carry):
-        pl.semaphore_signal(
-            barrier, inc=1, device_id={"depth": (d + k) % DEPTHS}, device_id_type=MESH
-        )
-        return carry
-
-    lax.fori_loop(1, DEPTHS, greet, 0)
+    @pl.when(d > 0)
+    def _():
+        pl.semaphore_signal(barrier, inc=1, device_id={"depth": d - 1}, device_id_type=MESH)
 
     def build():
         def one_lag(lag, carry):
@@ -67,49 +81,77 @@
 
     @pl.when(d == 0)
     def _():
-        inbuf[...] = x_ref[...]
+        shot = lax.broadcasted_iota(jnp.int32, (SHOTS, SHOTS), 0)
+        chosen = jnp.where(shot == shot_ref[...], 1.0, 0.0).astype(BF16)
+        ways = [expand(0), expand(1)]
+        contract = (((0,), (0,)), ((), ()))
+        packed = []
+        for kind in range(2):
+            total = None
+            for half in range(2):
+                way = ways[half]
+                if kind == 0:
+                    way = jnp.dot(chosen, way, preferred_element_type=F32).astype(BF16)
+                term = lax.dot_general(
+                    way, x_ref[kind, half], contract, preferred_element_type=F32
+                )
+                total = term if total is None else total + term
+            packed.append(total.reshape(BATCHES, HALF, POINTS))
+        inbuf[...] = jnp.concatenate(packed, axis=1).astype(BF16)
 
     load_e.wait()
-    pl.semaphore_wait(barrier, 4 + DEPTHS - 1)
+
+    @pl.when(d < DEPTHS - 1)
+    def _():
+        pl.semaphore_wait(barrier, 5)
+
+    @pl.when(d == DEPTHS - 1)
+    def _():
+        pl.semaphore_wait(barrier, 4)
 
     def hop(b):
-        rows = pl.ds(pl.multiple_of(b * HALF, HALF), HALF)
         return pltpu.make_async_remote_copy(
-            src_ref=fin.at[:, rows, :],
-            dst_ref=inbuf.at[:, rows, :],
+            src_ref=fin.at[b],
+            dst_ref=inbuf.at[b],
             send_sem=chain_send.at[b],
             recv_sem=chain_recv.at[b],
             device_id={"depth": d + 1},
             device_id_type=MESH,
         )
 
-    def step(b, carry):
-        rows = pl.ds(pl.multiple_of(b * HALF, HALF), HALF)
-
+    def step(b):
         @pl.when(d > 0)
         def _():
             hop(b).wait_recv()
 
-        values = inbuf[:, rows, :].reshape(2 * HALF, POINTS)
+        values = inbuf[b]
         first = jnp.dot(values, e_ref[0], preferred_element_type=F32)
         second = jnp.dot(values, e_ref[1], preferred_element_type=F32)
-        m = BATCH
-        source = jnp.concatenate(
-            [first[:m] - second[m : 2 * m], second[:m] + first[m : 2 * m]], axis=0
-        )
-        record = jnp.concatenate(
-            [first[2 * m : 3 * m] + second[3 * m :], first[3 * m :] - second[2 * m : 3 * m]], axis=0
-        )
-        fin[0, rows, :] = source.astype(BF16)
-        fin[1, rows, :] = record.astype(BF16)
+        result = swap_parts(first, second)
+        fin[b] = result.astype(BF16)
 
         @pl.when(d < DEPTHS - 1)
         def _():
             hop(b).start()
 
-        return carry
-
-    lax.fori_loop(0, BATCHES, step, 0)
+        return result
+
+    def two_steps(p, carry):
+        even = step(2 * p)
+        odd = step(2 * p + 1)
+        rows = pl.ds(pl.multiple_of(p * 2 * HALF, 2 * HALF), 2 * HALF)
+        field[0, rows, :] = jnp.concatenate([even[:HALF], odd[:HALF]], axis=0).astype(BF16)
+        field[1, rows, :] = jnp.concatenate([even[HALF:], odd[HALF:]], axis=0).astype(BF16)
+        return carry
+
+    two_steps(0, 0)
+
+    def greet(k, carry):
+        pl.semaphore_signal(greet_sem, inc=1, device_id={"depth": k}, device_id_type=MESH)
+        return carry
+
+    lax.fori_loop(0, d, greet, 0)
+    lax.fori_loop(1, BATCHES // 2, two_steps, 0)
 
     mine = pl.ds(pl.multiple_of(core * ROWS, ROWS), ROWS)
     theirs = pl.ds(pl.multiple_of((1 - core) * ROWS, ROWS), ROWS)
@@ -129,7 +171,7 @@
         block = (yh + q * (1 - 2 * yh)) * 4 + (x + r) % 4
         columns = pl.ds(pl.multiple_of(block * 2 * ROWS, 2 * ROWS), 2 * ROWS)
         term = lax.dot_general(
-            fin[0, :, columns], fin[1], (((0,), (0,)), ((), ())), preferred_element_type=F32
+            field[0, :, columns], field[1], (((0,), (0,)), ((), ())), preferred_element_type=F32
         )
         part[t] = (term * factor).astype(BF16)
         to_core(t).start()
@@ -242,6 +284,11 @@
         deal(k).start()
         return carry
 
+
+    @pl.when(d < DEPTHS - 1)
+    def _():
+        pl.semaphore_wait(greet_sem, DEPTHS - 1 - d)
+
     lax.fori_loop(1, DEPTHS, send_piece, 0)
     gath[d] = pieces[d]
 
@@ -290,7 +337,7 @@
     lax.fori_loop(1, DEPTHS, drain_piece, 0)
 
 
-def migrate(extrap, packed, factor, angle_lag):
+def migrate(extrap, fields, shots, factor, angle_lag):
     vmem = pl.BlockSpec(memory_space=pltpu.VMEM)
     return pl.pallas_call(
         kernel,
@@ -298,13 +345,15 @@
         in_specs=[
             pl.BlockSpec(memory_space=pl.ANY),
             vmem,
+            vmem,
             pl.BlockSpec(memory_space=pltpu.SMEM),
             vmem,
         ],
         out_specs=vmem,
         scratch_shapes=[
             pltpu.VMEM((2, POINTS, POINTS), BF16),
-            pltpu.VMEM((2, 2 * SHOTS, POINTS), BF16),
+            pltpu.VMEM((BATCHES, 2 * HALF, POINTS), BF16),
+            pltpu.VMEM((BATCHES, 2 * HALF, POINTS), BF16),
             pltpu.VMEM((2, 2 * SHOTS, POINTS), BF16),
             pltpu.VMEM((DEPTHS, POINTS, ANGLES), BF16),
             pltpu.VMEM((8, 2 * ROWS, POINTS), BF16),
@@ -334,27 +383,22 @@
             pltpu.SemaphoreType.DMA,
             pltpu.SemaphoreType.DMA((DEPTHS,)),
             pltpu.SemaphoreType.DMA((DEPTHS,)),
+            pltpu.SemaphoreType.REGULAR,
         ],
         compiler_params=pltpu.CompilerParams(
             collective_id=0, has_side_effects=True, vmem_limit_bytes=48 * 1024 * 1024
         ),
         name="migrate",
-    )(extrap, packed, factor, angle_lag)
+    )(extrap, fields, shots, factor, angle_lag)
 
 
 def shards(extrap, source_field, record_field, shot_of_record, freq_index, angle_lag):
     freq_count = lax.axis_size("freq")
-    paired = source_field[0].at[shot_of_record].get(mode="promise_in_bounds")
-
-    def pack(field):
-        split = field.reshape(BATCHES, BATCH, 2, POINTS)
-        return split.transpose(0, 2, 1, 3).reshape(2 * SHOTS, POINTS)
-
-    packed = jnp.stack([pack(paired), pack(record_field[0])])
+    fields = jnp.stack([source_field[0], record_field[0]]).transpose(0, 2, 1, 3)
     factor = (
         (freq_index.astype(F32) + 1.0) / (8 * freq_count) / math.sqrt(SHOTS * freq_count)
     )
-    return migrate(extrap[0, 0], packed, factor, angle_lag)
+    return migrate(extrap[0, 0], fields, shot_of_record.reshape(1, SHOTS), factor, angle_lag)
 
 
 def solution(mesh):

time: 129 us -> 115 us (0.89)
  Pallas kernels: 124 us -> 111 us
    pallas_call x1, Pallas kernels: 124 us -> 111 us  [migrate(): pl.pallas_call(kernel, out_shape=jax.ShapeDtypeStruct((PIECE, DEPTHS, ANG...]
    unnamed x5 -> x7, local copies, waits for them, and re-layouts: 0.91 us -> 3.03 us
    gather x1 -> x0, local copies, waits for them, and re-layouts: 1.62 us -> none  [shards(): paired = source_field[0].at[shot_of_record].get(mode='promise_in_bounds')]
where the time goes in v3:
time: 115 us
  Pallas kernels  111 us (97%)
  local copies, waits for them, and re-layouts  3.03 us (3%)
    pallas_call x1, Pallas kernels, migrate(): pl.pallas_call(kernel, out_shape=jax.ShapeDtypeStruct((PIECE, DEPTHS, ANG...  111 us
    unnamed x7, local copies, waits for them, and re-layouts  3.03 us

profile of v3, /device:TPU:32, one launch (start us, length us, event | category | flops | bytes accessed | tf_op | source)
XLA Modules:
  0.0 115.3 jit_solution(9496530088536629593)
XLA Ops:
  0.0 0.0 copy-start.1
  0.0 0.0 copy-start
  0.0 1.2 %copy.7 = bf16[1,128,2,1024]{3,1,2,0:T(8,128)(2,1)S(1)} copy(bf16[1,128,2,1024]{3,2,1,0:T(2,128)(2,1)} %param.7) | data formatting | bytes 1048576 | tf_op args[1]
  1.3 1.2 copy.8
  2.4 0.1 maximum_bitcast_fusion.x_ref
  3.2 0.0 copy-done.1
  3.2 0.0 copy-done
  3.2 111.5 %migrate.1 = f32[4,16,256]{2,1,0:T(8,128)S(1)} custom-call(bf16[2,1024,1024]{2,1,0:T(8,128)(2,1)} %bitcast.5, bf16[2,2,128,1024]{3,2,1,0:T(8,128)(2,1)S(1)} %maximum_bitcast_fusion.x_ref, s32[1,128]{1,0:T(1,128)S(1)} %bitcast.4, f32[1]{0:T(128)S(6)} %div.4.factor_ref, s32[1024,256]{1,0:T(8,128)S(1)} %copy-done), custom_call_target="tpu_custom_call" | custom-call | tf_op jit(solution)/shard_map/migrate/pallas_call | solution.py:342
  114.7 0.6 copy.11
Async XLA Ops:
  0.0 3.2 %copy-start.1 = (s32[128]{0:T(128)S(1)}, s32[128]{0:T(128)}, u32[]{:S(2)}) copy-start(s32[128]{0:T(128)} %param.9) | copy-start | bytes 1540
  0.0 3.2 %copy-start = (s32[1024,256]{1,0:T(8,128)S(1)}, s32[1024,256]{1,0:T(8,128)}, u32[]{:S(2)}) copy-start(s32[1024,256]{1,0:T(8,128)} %lag_ref.1) | copy-start | bytes 3145732

commit v4 on v3

--- a/solution.py
+++ b/solution.py
@@ -36,16 +36,26 @@
     shape = (SHOTS, 2 * SHOTS)
     shot = lax.broadcasted_iota(jnp.int32, shape, 0)
     row = lax.broadcasted_iota(jnp.int32, shape, 1)
-    place = row - BATCH * part
-    hit = (place >= 0) & (place % HALF < BATCH) & ((place // HALF) * BATCH + place % HALF == shot)
+    hit = ((row // HALF) * BATCH + row % BATCH == shot) & ((row % HALF) // BATCH == part)
     return jnp.where(hit, 1.0, 0.0).astype(BF16)
 
 
+def spread(shots, part):
+    line = lax.broadcasted_iota(jnp.int32, (2 * SHOTS, SHOTS), 0)
+    return jnp.where(2 * shots + part == line, 1.0, 0.0).astype(BF16)
+
+
+def route(shots):
+    total = jnp.dot(spread(shots, 0), expand(0), preferred_element_type=F32)
+    total = total + jnp.dot(spread(shots, 1), expand(1), preferred_element_type=F32)
+    return total.astype(BF16)
+
+
 def kernel(
-    e_hbm, x_ref, shot_ref, factor_ref, lag_ref, out_ref,
-    e_ref, inbuf, fin, field, sel, part, corein, two, one, three, rel_up, rel_down, from_down, from_up,
+    e_hbm, source_hbm, record_hbm, shot_hbm, factor_ref, lag_hbm, out_ref,
+    e_ref, source_ref, record_ref, shot_ref, lag_ref, inbuf, fin, field, sel, part, corein, two, one, three, rel_up, rel_down, from_down, from_up,
     ysend, yin, acc, pieces, gath, xs, g,
-    e_sem, chain_send, chain_recv, core_send, core_recv, x_send, x_recv, y_send, y_recv, d_send, d_recv, greet_sem,
+    e_sem, lag_sem, raw_sem, chain_send, chain_recv, core_send, core_recv, x_send, x_recv, y_send, y_recv, d_send, d_recv, greet_sem,
 ):
     d = lax.axis_index("depth")
     f = lax.axis_index("freq")
@@ -59,6 +69,19 @@
 
     load_e = pltpu.make_async_copy(e_hbm, e_ref, e_sem)
     load_e.start()
+    load_lag = pltpu.make_async_copy(lag_hbm, lag_ref, lag_sem)
+    load_lag.start()
+    raw = [
+        pltpu.make_async_copy(shot_hbm, shot_ref, raw_sem.at[0]),
+        pltpu.make_async_copy(source_hbm, source_ref, raw_sem.at[1]),
+        pltpu.make_async_copy(record_hbm, record_ref, raw_sem.at[2]),
+    ]
+
+    @pl.when(d == 0)
+    def _():
+        for load in raw:
+            load.start()
+
     barrier = pltpu.get_barrier_semaphore()
     for other in (partner, up, down, across):
         pl.semaphore_signal(barrier, inc=1, device_id={"freq": other}, device_id_type=MESH)
@@ -68,6 +91,8 @@
         pl.semaphore_signal(barrier, inc=1, device_id={"depth": d - 1}, device_id_type=MESH)
 
     def build():
+        load_lag.wait()
+
         def one_lag(lag, carry):
             sel[lag] = jnp.where(lag_ref[...] == lag, 1.0, 0.0).astype(BF16)
             g[lag, :, ROWS:, :] = jnp.zeros((2, ROWS, LANES), F32)
@@ -81,22 +106,16 @@
 
     @pl.when(d == 0)
     def _():
-        shot = lax.broadcasted_iota(jnp.int32, (SHOTS, SHOTS), 0)
-        chosen = jnp.where(shot == shot_ref[...], 1.0, 0.0).astype(BF16)
-        ways = [expand(0), expand(1)]
-        contract = (((0,), (0,)), ((), ()))
+        for load in raw:
+            load.wait()
+        straight = lax.broadcasted_iota(jnp.int32, (1, SHOTS), 1)
         packed = []
-        for kind in range(2):
-            total = None
-            for half in range(2):
-                way = ways[half]
-                if kind == 0:
-                    way = jnp.dot(chosen, way, preferred_element_type=F32).astype(BF16)
-                term = lax.dot_general(
-                    way, x_ref[kind, half], contract, preferred_element_type=F32
-                )
-                total = term if total is None else total + term
-            packed.append(total.reshape(BATCHES, HALF, POINTS))
+        for field_ref, shots in ((source_ref, shot_ref[...]), (record_ref, straight)):
+            lines = field_ref[...].reshape(2 * SHOTS, POINTS)
+            rows = lax.dot_general(
+                route(shots), lines, (((0,), (0,)), ((), ())), preferred_element_type=F32
+            )
+            packed.append(rows.reshape(BATCHES, HALF, POINTS))
         inbuf[...] = jnp.concatenate(packed, axis=1).astype(BF16)
 
     load_e.wait()
@@ -109,12 +128,16 @@
     def _():
         pl.semaphore_wait(barrier, 4)
 
-    def hop(b):
+    side = POINTS // 2
+    sides = [slice(0, side), slice(side, POINTS)]
+
+    def hop(b, n):
+        columns = pl.ds(n * side, side)
         return pltpu.make_async_remote_copy(
-            src_ref=fin.at[b],
-            dst_ref=inbuf.at[b],
-            send_sem=chain_send.at[b],
-            recv_sem=chain_recv.at[b],
+            src_ref=fin.at[b, :, columns],
+            dst_ref=inbuf.at[b, :, columns],
+            send_sem=chain_send.at[2 * b + n],
+            recv_sem=chain_recv.at[2 * b + n],
             device_id={"depth": d + 1},
             device_id_type=MESH,
         )
@@ -122,26 +145,46 @@
     def step(b):
         @pl.when(d > 0)
         def _():
-            hop(b).wait_recv()
-
-        values = inbuf[b]
-        first = jnp.dot(values, e_ref[0], preferred_element_type=F32)
-        second = jnp.dot(values, e_ref[1], preferred_element_type=F32)
-        result = swap_parts(first, second)
-        fin[b] = result.astype(BF16)
-
-        @pl.when(d < DEPTHS - 1)
+            hop(b, 0).wait_recv()
+
+        values = inbuf[b, :, sides[0]]
+        first = jnp.dot(values, e_ref[0, sides[0], :], preferred_element_type=F32)
+        second = jnp.dot(values, e_ref[1, sides[0], :], preferred_element_type=F32)
+
+        @pl.when(d > 0)
         def _():
-            hop(b).start()
-
-        return result
+            hop(b, 1).wait_recv()
+
+        values = inbuf[b, :, sides[1]]
+        results = []
+        for n in range(2):
+            part_first = first[:, sides[n]] + jnp.dot(
+                values, e_ref[0, sides[1], sides[n]], preferred_element_type=F32
+            )
+            part_second = second[:, sides[n]] + jnp.dot(
+                values, e_ref[1, sides[1], sides[n]], preferred_element_type=F32
+            )
+            result = swap_parts(part_first, part_second)
+            fin[b, :, sides[n]] = result.astype(BF16)
+
+            @pl.when(d < DEPTHS - 1)
+            def _():
+                hop(b, n).start()
+
+            results.append(result)
+        return results
 
     def two_steps(p, carry):
         even = step(2 * p)
         odd = step(2 * p + 1)
         rows = pl.ds(pl.multiple_of(p * 2 * HALF, 2 * HALF), 2 * HALF)
-        field[0, rows, :] = jnp.concatenate([even[:HALF], odd[:HALF]], axis=0).astype(BF16)
-        field[1, rows, :] = jnp.concatenate([even[HALF:], odd[HALF:]], axis=0).astype(BF16)
+        for n in range(2):
+            field[0, rows, sides[n]] = jnp.concatenate(
+                [even[n][:HALF], odd[n][:HALF]], axis=0
+            ).astype(BF16)
+            field[1, rows, sides[n]] = jnp.concatenate(
+                [even[n][HALF:], odd[n][HALF:]], axis=0
+            ).astype(BF16)
         return carry
 
     two_steps(0, 0)
@@ -309,16 +352,17 @@
     lax.fori_loop(0, DEPTHS, stack, 0)
     scale = 1.0 / math.sqrt(POINTS)
     for row in range(PIECE):
-        for side in range(2):
-            total = g[0, side, pl.ds(row, DEPTHS, stride=PIECE), :]
+        for wing in range(2):
+            total = g[0, wing, pl.ds(row, DEPTHS, stride=PIECE), :]
             for lag in range(1, DEPTHS):
-                total = total + g[lag, side, pl.ds(PIECE * lag + row, DEPTHS, stride=PIECE), :]
-            out_ref[row, :, LANES * side : LANES * (side + 1)] = total * scale
+                total = total + g[lag, wing, pl.ds(PIECE * lag + row, DEPTHS, stride=PIECE), :]
+            out_ref[row, :, LANES * wing : LANES * (wing + 1)] = total * scale
 
     @pl.when(d < DEPTHS - 1)
     def _():
         def drain(b, carry):
-            hop(b).wait_send()
+            hop(b, 0).wait_send()
+            hop(b, 1).wait_send()
             return carry
 
         lax.fori_loop(0, BATCHES, drain, 0)
@@ -337,21 +381,20 @@
     lax.fori_loop(1, DEPTHS, drain_piece, 0)
 
 
-def migrate(extrap, fields, shots, factor, angle_lag):
+def migrate(extrap, source, record, shots, factor, angle_lag):
     vmem = pl.BlockSpec(memory_space=pltpu.VMEM)
+    hbm = pl.BlockSpec(memory_space=pltpu.HBM)
     return pl.pallas_call(
         kernel,
         out_shape=jax.ShapeDtypeStruct((PIECE, DEPTHS, ANGLES), F32),
-        in_specs=[
-            pl.BlockSpec(memory_space=pl.ANY),
-            vmem,
-            vmem,
-            pl.BlockSpec(memory_space=pltpu.SMEM),
-            vmem,
-        ],
+        in_specs=[hbm, hbm, hbm, hbm, pl.BlockSpec(memory_space=pltpu.SMEM), hbm],
         out_specs=vmem,
         scratch_shapes=[
             pltpu.VMEM((2, POINTS, POINTS), BF16),
+            pltpu.VMEM((SHOTS, 2, POINTS), BF16),
+            pltpu.VMEM((SHOTS, 2, POINTS), BF16),
+            pltpu.VMEM((1, SHOTS), jnp.int32),
+            pltpu.VMEM((POINTS, ANGLES), jnp.int32),
             pltpu.VMEM((BATCHES, 2 * HALF, POINTS), BF16),
             pltpu.VMEM((BATCHES, 2 * HALF, POINTS), BF16),
             pltpu.VMEM((2, 2 * SHOTS, POINTS), BF16),
@@ -373,8 +416,10 @@
             pltpu.VMEM((ROWS, POINTS), F32),
             pltpu.VMEM((DEPTHS, 2, 2 * ROWS, LANES), F32),
             pltpu.SemaphoreType.DMA,
-            pltpu.SemaphoreType.DMA((BATCHES,)),
-            pltpu.SemaphoreType.DMA((BATCHES,)),
+            pltpu.SemaphoreType.DMA,
+            pltpu.SemaphoreType.DMA((3,)),
+            pltpu.SemaphoreType.DMA((2 * BATCHES,)),
+            pltpu.SemaphoreType.DMA((2 * BATCHES,)),
             pltpu.SemaphoreType.DMA((8,)),
             pltpu.SemaphoreType.DMA((8,)),
             pltpu.SemaphoreType.DMA((12,)),
@@ -386,19 +431,21 @@
             pltpu.SemaphoreType.REGULAR,
         ],
         compiler_params=pltpu.CompilerParams(
-            collective_id=0, has_side_effects=True, vmem_limit_bytes=48 * 1024 * 1024
+            collective_id=0, has_side_effects=True, vmem_limit_bytes=67043328 - 200 * 1024
         ),
         name="migrate",
-    )(extrap, fields, shots, factor, angle_lag)
+    )(extrap, source, record, shots, factor, angle_lag)
 
 
 def shards(extrap, source_field, record_field, shot_of_record, freq_index, angle_lag):
     freq_count = lax.axis_size("freq")
-    fields = jnp.stack([source_field[0], record_field[0]]).transpose(0, 2, 1, 3)
+    shots = shot_of_record.reshape(1, SHOTS)
     factor = (
         (freq_index.astype(F32) + 1.0) / (8 * freq_count) / math.sqrt(SHOTS * freq_count)
     )
-    return migrate(extrap[0, 0], fields, shot_of_record.reshape(1, SHOTS), factor, angle_lag)
+    return migrate(
+        extrap[0, 0], source_field[0], record_field[0], shots, factor, angle_lag
+    )
 
 
 def solution(mesh):

time: 115 us -> 114 us (level)
  local copies, waits for them, and re-layouts: 3.03 us -> 1.47 us
    unnamed x7 -> x1, local copies, waits for them, and re-layouts: 3.03 us -> 1.47 us
where the time goes in v4:
time: 114 us
  Pallas kernels  112 us (98%)
  local copies, waits for them, and re-layouts  1.47 us (1%)
    pallas_call x1, Pallas kernels, migrate(): pl.pallas_call(kernel, out_shape=jax.ShapeDtypeStruct((PIECE, DEPTHS, ANG...  112 us

profile of v4, /device:TPU:32, one launch (start us, length us, event | category | flops | bytes accessed | tf_op | source)
XLA Modules:
  0.0 114.0 jit_solution(10329768974732224248)
XLA Ops:
  0.7 111.9 %migrate.1 = f32[4,16,256]{2,1,0:T(8,128)} custom-call(bf16[2,1024,1024]{2,1,0:T(8,128)(2,1)} %bitcast.4, bf16[128,2,1024]{2,1,0:T(2,128)(2,1)} %bitcast.5, bf16[128,2,1024]{2,1,0:T(2,128)(2,1)} %bitcast.6, s32[1,128]{1,0:T(1,128)} %bitcast.7, f32[1]{0:T(128)S(6)} %div.4.factor_ref, s32[1024,256]{1,0:T(8,128)} %lag_hbm.1), custom_call_target="tpu_custom_call" | custom-call | tf_op jit(solution)/shard_map/migrate/pallas_call | solution.py:387
  112.5 1.5 %copy.9 = f32[4,16,256]{2,1,0:T(8,128)} copy(f32[4,16,256]{2,1,0:T(8,128)} %migrate.1) | data formatting | bytes 131072

commit v5 on v4

--- a/solution.py
+++ b/solution.py
@@ -68,9 +68,7 @@
     across = f + 8 - 16 * yh
 
     load_e = pltpu.make_async_copy(e_hbm, e_ref, e_sem)
-    load_e.start()
     load_lag = pltpu.make_async_copy(lag_hbm, lag_ref, lag_sem)
-    load_lag.start()
     raw = [
         pltpu.make_async_copy(shot_hbm, shot_ref, raw_sem.at[0]),
         pltpu.make_async_copy(source_hbm, source_ref, raw_sem.at[1]),
@@ -82,6 +80,8 @@
         for load in raw:
             load.start()
 
+    load_e.start()
+    load_lag.start()
     barrier = pltpu.get_barrier_semaphore()
     for other in (partner, up, down, across):
         pl.semaphore_signal(barrier, inc=1, device_id={"freq": other}, device_id_type=MESH)
@@ -431,7 +431,7 @@
             pltpu.SemaphoreType.REGULAR,
         ],
         compiler_params=pltpu.CompilerParams(
-            collective_id=0, has_side_effects=True, vmem_limit_bytes=67043328 - 200 * 1024
+            collective_id=0, has_side_effects=True, vmem_limit_bytes=67043328 - 10400 * 1024
         ),
         name="migrate",
     )(extrap, source, record, shots, factor, angle_lag)

time: 114 us -> 112 us (0.982)
  Pallas kernels: 112 us -> 110 us
    pallas_call x1, Pallas kernels: 112 us -> 110 us  [migrate(): pl.pallas_call(kernel, out_shape=jax.ShapeDtypeStruct((PIECE, DEPTHS, ANG...]
where the time goes in v5:
time: 112 us
  Pallas kernels  110 us (98%)
  local copies, waits for them, and re-layouts  1.28 us (1%)
    pallas_call x1, Pallas kernels, migrate(): pl.pallas_call(kernel, out_shape=jax.ShapeDtypeStruct((PIECE, DEPTHS, ANG...  110 us

profile of v5, /device:TPU:32, one launch (start us, length us, event | category | flops | bytes accessed | tf_op | source)
XLA Modules:
  0.0 111.6 jit_solution(6347568398764348588)
XLA Ops:
  0.7 0.0 copy-start
  0.7 0.6 copy-done
  1.3 109.7 %migrate.1 = f32[4,16,256]{2,1,0:T(8,128)S(1)} custom-call(bf16[2,1024,1024]{2,1,0:T(8,128)(2,1)} %bitcast.5, bf16[128,2,1024]{2,1,0:T(2,128)(2,1)} %bitcast.6, bf16[128,2,1024]{2,1,0:T(2,128)(2,1)} %bitcast.7, s32[1,128]{1,0:T(1,128)S(1)} %bitcast.4, f32[1]{0:T(128)S(6)} %div.4.factor_ref, s32[1024,256]{1,0:T(8,128)} %lag_hbm.1), custom_call_target="tpu_custom_call" | custom-call | tf_op jit(solution)/shard_map/migrate/pallas_call | solution.py:387
  111.0 0.6 copy.9
Async XLA Ops:
  0.7 0.7 copy-start

commit v6 on v5

--- a/solution.py
+++ b/solution.py
@@ -15,6 +15,7 @@
 ANGLES = 256
 SHOTS = 128
 LANES = 128
+GROUP = 4
 BATCHES = SHOTS // BATCH
 HALF = 2 * BATCH
 PIECE = ROWS // DEPTHS
@@ -54,7 +55,7 @@
 def kernel(
     e_hbm, source_hbm, record_hbm, shot_hbm, factor_ref, lag_hbm, out_ref,
     e_ref, source_ref, record_ref, shot_ref, lag_ref, inbuf, fin, field, sel, part, corein, two, one, three, rel_up, rel_down, from_down, from_up,
-    ysend, yin, acc, pieces, gath, xs, g,
+    ysend, yin, acc, pieces, gath, xs, xb, g,
     e_sem, lag_sem, raw_sem, chain_send, chain_recv, core_send, core_recv, x_send, x_recv, y_send, y_recv, d_send, d_recv, greet_sem,
 ):
     d = lax.axis_index("depth")
@@ -343,13 +344,17 @@
     for k in range(DEPTHS):
         xs[PIECE * k : PIECE * (k + 1), :] = gath[k].astype(F32)
 
-    def stack(lag, carry):
-        term = jnp.dot(xs[...].astype(BF16), sel[lag], preferred_element_type=F32)
-        g[lag, 0, 0:ROWS, :] = term[:, :LANES]
-        g[lag, 1, 0:ROWS, :] = term[:, LANES:]
-        return carry
-
-    lax.fori_loop(0, DEPTHS, stack, 0)
+    xb[...] = xs[...].astype(BF16)
+
+    def stack(p, carry):
+        lags = [GROUP * p + k for k in range(GROUP)]
+        terms = [jnp.dot(xb[...], sel[lag], preferred_element_type=F32) for lag in lags]
+        for lag, term in zip(lags, terms):
+            g[lag, 0, 0:ROWS, :] = term[:, :LANES]
+            g[lag, 1, 0:ROWS, :] = term[:, LANES:]
+        return carry
+
+    lax.fori_loop(0, DEPTHS // GROUP, stack, 0)
     scale = 1.0 / math.sqrt(POINTS)
     for row in range(PIECE):
         for wing in range(2):
@@ -414,6 +419,7 @@
             pltpu.VMEM((DEPTHS, PIECE, POINTS), BF16),
             pltpu.VMEM((DEPTHS, PIECE, POINTS), BF16),
             pltpu.VMEM((ROWS, POINTS), F32),
+            pltpu.VMEM((ROWS, POINTS), BF16),
             pltpu.VMEM((DEPTHS, 2, 2 * ROWS, LANES), F32),
             pltpu.SemaphoreType.DMA,
             pltpu.SemaphoreType.DMA,

time: 112 us -> 110 us (0.982)
  Pallas kernels: 110 us -> 108 us
    pallas_call x1, Pallas kernels: 110 us -> 108 us  [migrate(): pl.pallas_call(kernel, out_shape=jax.ShapeDtypeStruct((PIECE, DEPTHS, ANG...]
where the time goes in v6:
time: 110 us
  Pallas kernels  108 us (98%)
  local copies, waits for them, and re-layouts  1.28 us (1%)
    pallas_call x1, Pallas kernels, migrate(): pl.pallas_call(kernel, out_shape=jax.ShapeDtypeStruct((PIECE, DEPTHS, ANG...  108 us

profile of v6, /device:TPU:32, one launch (start us, length us, event | category | flops | bytes accessed | tf_op | source)
XLA Modules:
  0.0 110.2 jit_solution(15020906571723207892)
XLA Ops:
  0.7 0.0 copy-start
  0.7 0.6 copy-done
  1.3 108.2 %migrate.1 = f32[4,16,256]{2,1,0:T(8,128)S(1)} custom-call(bf16[2,1024,1024]{2,1,0:T(8,128)(2,1)} %bitcast.5, bf16[128,2,1024]{2,1,0:T(2,128)(2,1)} %bitcast.6, bf16[128,2,1024]{2,1,0:T(2,128)(2,1)} %bitcast.7, s32[1,128]{1,0:T(1,128)S(1)} %bitcast.4, f32[1]{0:T(128)S(6)} %div.4.factor_ref, s32[1024,256]{1,0:T(8,128)} %lag_hbm.1), custom_call_target="tpu_custom_call" | custom-call | tf_op jit(solution)/shard_map/migrate/pallas_call | solution.py:392
  109.6 0.6 copy.9
Async XLA Ops:
  0.7 0.7 copy-start

commit v7 on v6

--- a/solution.py
+++ b/solution.py
@@ -55,8 +55,8 @@
 def kernel(
     e_hbm, source_hbm, record_hbm, shot_hbm, factor_ref, lag_hbm, out_ref,
     e_ref, source_ref, record_ref, shot_ref, lag_ref, inbuf, fin, field, sel, part, corein, two, one, three, rel_up, rel_down, from_down, from_up,
-    ysend, yin, acc, pieces, gath, xs, xb, g,
-    e_sem, lag_sem, raw_sem, chain_send, chain_recv, core_send, core_recv, x_send, x_recv, y_send, y_recv, d_send, d_recv, greet_sem,
+    acc, pieces, gath, xs, xb, g,
+    e_sem, lag_sem, raw_sem, chain_send, chain_recv, core_send, core_recv, x_send, x_recv, d_send, d_recv, greet_sem,
 ):
     d = lax.axis_index("depth")
     f = lax.axis_index("freq")
@@ -68,7 +68,14 @@
     down = yh * 8 + ((x + 3) % 4) * 2 + core
     across = f + 8 - 16 * yh
 
-    load_e = pltpu.make_async_copy(e_hbm, e_ref, e_sem)
+    side = POINTS // 2
+    sides = [slice(0, side), slice(side, POINTS)]
+    load_e = [
+        pltpu.make_async_copy(
+            e_hbm.at[:, pl.ds(n * side, side), :], e_ref.at[:, pl.ds(n * side, side), :], e_sem.at[n]
+        )
+        for n in range(2)
+    ]
     load_lag = pltpu.make_async_copy(lag_hbm, lag_ref, lag_sem)
     raw = [
         pltpu.make_async_copy(shot_hbm, shot_ref, raw_sem.at[0]),
@@ -81,7 +88,8 @@
         for load in raw:
             load.start()
 
-    load_e.start()
+    for load in load_e:
+        load.start()
     load_lag.start()
     barrier = pltpu.get_barrier_semaphore()
     for other in (partner, up, down, across):
@@ -119,8 +127,6 @@
             packed.append(rows.reshape(BATCHES, HALF, POINTS))
         inbuf[...] = jnp.concatenate(packed, axis=1).astype(BF16)
 
-    load_e.wait()
-
     @pl.when(d < DEPTHS - 1)
     def _():
         pl.semaphore_wait(barrier, 5)
@@ -128,9 +134,6 @@
     @pl.when(d == DEPTHS - 1)
     def _():
         pl.semaphore_wait(barrier, 4)
-
-    side = POINTS // 2
-    sides = [slice(0, side), slice(side, POINTS)]
 
     def hop(b, n):
         columns = pl.ds(n * side, side)
@@ -143,7 +146,10 @@
             device_id_type=MESH,
         )
 
-    def step(b):
+    def step(b, first_step=False):
+        if first_step:
+            load_e[0].wait()
+
         @pl.when(d > 0)
         def _():
             hop(b, 0).wait_recv()
@@ -156,6 +162,8 @@
         def _():
             hop(b, 1).wait_recv()
 
+        if first_step:
+            load_e[1].wait()
         values = inbuf[b, :, sides[1]]
         results = []
         for n in range(2):
@@ -175,8 +183,8 @@
             results.append(result)
         return results
 
-    def two_steps(p, carry):
-        even = step(2 * p)
+    def two_steps(p, carry, first_step=False):
+        even = step(2 * p, first_step)
         odd = step(2 * p + 1)
         rows = pl.ds(pl.multiple_of(p * 2 * HALF, 2 * HALF), 2 * HALF)
         for n in range(2):
@@ -188,10 +196,13 @@
             ).astype(BF16)
         return carry
 
-    two_steps(0, 0)
+    two_steps(0, 0, True)
 
     def greet(k, carry):
-        pl.semaphore_signal(greet_sem, inc=1, device_id={"depth": k}, device_id_type=MESH)
+        for peer in (f, across):
+            pl.semaphore_signal(
+                greet_sem, inc=1, device_id={"depth": k, "freq": peer}, device_id_type=MESH
+            )
         return carry
 
     lax.fori_loop(0, d, greet, 0)
@@ -211,14 +222,17 @@
         )
 
     factor = factor_ref[0]
-    for t, (q, r) in enumerate(ORDER):
-        block = (yh + q * (1 - 2 * yh)) * 4 + (x + r) % 4
-        columns = pl.ds(pl.multiple_of(block * 2 * ROWS, 2 * ROWS), 2 * ROWS)
-        term = lax.dot_general(
-            field[0, :, columns], field[1], (((0,), (0,)), ((), ())), preferred_element_type=F32
-        )
-        part[t] = (term * factor).astype(BF16)
-        to_core(t).start()
+    for pair_start in range(0, len(ORDER), 2):
+        for t in (pair_start, pair_start + 1):
+            q, r = ORDER[t]
+            block = (yh + q * (1 - 2 * yh)) * 4 + (x + r) % 4
+            columns = pl.ds(pl.multiple_of(block * 2 * ROWS, 2 * ROWS), 2 * ROWS)
+            term = lax.dot_general(
+                field[0, :, columns], field[1], (((0,), (0,)), ((), ())), preferred_element_type=F32
+            )
+            part[t] = (term * factor).astype(BF16)
+        to_core(pair_start).start()
+        to_core(pair_start + 1).start()
 
     @pl.when(d == 0)
     def _():
@@ -284,65 +298,61 @@
             copies[q][name].wait_recv()
         return pair(t) + from_down[q].astype(F32) + from_up[q].astype(F32)
 
-    over = pltpu.make_async_remote_copy(
-        src_ref=ysend, dst_ref=yin, send_sem=y_send, recv_sem=y_recv,
-        device_id={"freq": across}, device_id_type=MESH,
-    )
     far(1)
     near(1)
     far(0)
     relay(1)
     near(0)
-    ysend[...] = collect(1).astype(BF16)
-    over.start()
     relay(0)
-    acc[...] = collect(0)
-    over.wait_recv()
-    acc[...] = acc[...] + yin[...].astype(F32)
-    for k in range(DEPTHS):
-        pieces[k] = acc[PIECE * k : PIECE * (k + 1), :].astype(BF16)
-
-    def deal(k):
+
+    def deal(q, k):
         target = (d + k) % DEPTHS
         return pltpu.make_async_remote_copy(
-            src_ref=pieces.at[target],
-            dst_ref=gath.at[d],
-            send_sem=d_send.at[k],
-            recv_sem=d_recv.at[k],
-            device_id={"depth": target},
+            src_ref=pieces.at[q, target],
+            dst_ref=gath.at[q, d],
+            send_sem=d_send.at[q, k],
+            recv_sem=d_recv.at[q, k],
+            device_id={"depth": target, "freq": across if q else f},
             device_id_type=MESH,
         )
 
-    def arrival(k):
+    def arrival(q, k):
         source = (d + DEPTHS - k) % DEPTHS
         return pltpu.make_async_remote_copy(
-            src_ref=pieces.at[source],
-            dst_ref=gath.at[source],
-            send_sem=d_send.at[k],
-            recv_sem=d_recv.at[k],
-            device_id={"depth": source},
+            src_ref=pieces.at[q, source],
+            dst_ref=gath.at[q, source],
+            send_sem=d_send.at[q, k],
+            recv_sem=d_recv.at[q, k],
+            device_id={"depth": source, "freq": across if q else f},
             device_id_type=MESH,
         )
 
-    def send_piece(k, carry):
-        deal(k).start()
-        return carry
-
-
-    @pl.when(d < DEPTHS - 1)
-    def _():
-        pl.semaphore_wait(greet_sem, DEPTHS - 1 - d)
-
-    lax.fori_loop(1, DEPTHS, send_piece, 0)
-    gath[d] = pieces[d]
-
-    def take_piece(k, carry):
-        arrival(k).wait_recv()
-        return carry
-
-    lax.fori_loop(1, DEPTHS, take_piece, 0)
+    for q in (1, 0):
+        acc[...] = collect(q)
+        for k in range(DEPTHS):
+            pieces[q, k] = acc[PIECE * k : PIECE * (k + 1), :].astype(BF16)
+        if q:
+            @pl.when(d < DEPTHS - 1)
+            def _():
+                pl.semaphore_wait(greet_sem, 2 * (DEPTHS - 1 - d))
+
+        def send_piece(i, carry):
+            deal(q, DEPTHS // 2 + (i // 2 + i % 2) * (1 - 2 * (i % 2))).start()
+            return carry
+
+        lax.fori_loop(0, DEPTHS - 1, send_piece, 0)
+        if q:
+            deal(q, 0).start()
+    gath[0, d] = pieces[0, d]
+
+    for q in (1, 0):
+        def take_piece(k, carry):
+            arrival(q, k).wait_recv()
+            return carry
+
+        lax.fori_loop(1 - q, DEPTHS, take_piece, 0)
     for k in range(DEPTHS):
-        xs[PIECE * k : PIECE * (k + 1), :] = gath[k].astype(F32)
+        xs[PIECE * k : PIECE * (k + 1), :] = gath[0, k].astype(F32) + gath[1, k].astype(F32)
 
     xb[...] = xs[...].astype(BF16)
 
@@ -377,13 +387,12 @@
     for q in (0, 1):
         for copy in copies[q].values():
             copy.wait_send()
-    over.wait_send()
-
-    def drain_piece(k, carry):
-        deal(k).wait_send()
-        return carry
-
-    lax.fori_loop(1, DEPTHS, drain_piece, 0)
+    for q in (1, 0):
+        def drain_piece(k, carry):
+            deal(q, k).wait_send()
+            return carry
+
+        lax.fori_loop(1 - q, DEPTHS, drain_piece, 0)
 
 
 def migrate(extrap, source, record, shots, factor, angle_lag):
@@ -413,15 +422,13 @@
             pltpu.VMEM((2, ROWS // 2, POINTS), BF16),
             pltpu.VMEM((2, ROWS, POINTS), BF16),
             pltpu.VMEM((2, ROWS, POINTS), BF16),
-            pltpu.VMEM((ROWS, POINTS), BF16),
-            pltpu.VMEM((ROWS, POINTS), BF16),
             pltpu.VMEM((ROWS, POINTS), F32),
-            pltpu.VMEM((DEPTHS, PIECE, POINTS), BF16),
-            pltpu.VMEM((DEPTHS, PIECE, POINTS), BF16),
+            pltpu.VMEM((2, DEPTHS, PIECE, POINTS), BF16),
+            pltpu.VMEM((2, DEPTHS, PIECE, POINTS), BF16),
             pltpu.VMEM((ROWS, POINTS), F32),
             pltpu.VMEM((ROWS, POINTS), BF16),
             pltpu.VMEM((DEPTHS, 2, 2 * ROWS, LANES), F32),
-            pltpu.SemaphoreType.DMA,
+            pltpu.SemaphoreType.DMA((2,)),
             pltpu.SemaphoreType.DMA,
             pltpu.SemaphoreType.DMA((3,)),
             pltpu.SemaphoreType.DMA((2 * BATCHES,)),
@@ -430,10 +437,8 @@
             pltpu.SemaphoreType.DMA((8,)),
             pltpu.SemaphoreType.DMA((12,)),
             pltpu.SemaphoreType.DMA((12,)),
-            pltpu.SemaphoreType.DMA,
-            pltpu.SemaphoreType.DMA,
-            pltpu.SemaphoreType.DMA((DEPTHS,)),
-            pltpu.SemaphoreType.DMA((DEPTHS,)),
+            pltpu.SemaphoreType.DMA((2, DEPTHS)),
+            pltpu.SemaphoreType.DMA((2, DEPTHS)),
             pltpu.SemaphoreType.REGULAR,
         ],
         compiler_params=pltpu.CompilerParams(

time: 110 us -> 109 us (level)
    pallas_call x1, Pallas kernels: 108 us -> 107 us  [migrate(): pl.pallas_call(kernel, out_shape=jax.ShapeDtypeStruct((PIECE, DEPTHS, ANG...]
where the time goes in v7:
time: 109 us
  Pallas kernels  107 us (98%)
  local copies, waits for them, and re-layouts  1.28 us (1%)
    pallas_call x1, Pallas kernels, migrate(): pl.pallas_call(kernel, out_shape=jax.ShapeDtypeStruct((PIECE, DEPTHS, ANG...  107 us

profile of v7, /device:TPU:32, one launch (start us, length us, event | category | flops | bytes accessed | tf_op | source)
XLA Modules:
  0.0 108.6 jit_solution(14243268455663276242)
XLA Ops:
  0.7 0.0 copy-start
  0.7 0.6 copy-done
  1.3 106.7 %migrate.1 = f32[4,16,256]{2,1,0:T(8,128)S(1)} custom-call(bf16[2,1024,1024]{2,1,0:T(8,128)(2,1)} %bitcast.5, bf16[128,2,1024]{2,1,0:T(2,128)(2,1)} %bitcast.6, bf16[128,2,1024]{2,1,0:T(2,128)(2,1)} %bitcast.7, s32[1,128]{1,0:T(1,128)S(1)} %bitcast.4, f32[1]{0:T(128)S(6)} %div.4.factor_ref, s32[1024,256]{1,0:T(8,128)} %lag_hbm.1), custom_call_target="tpu_custom_call" | custom-call | tf_op jit(solution)/shard_map/migrate/pallas_call | solution.py:401
  108.0 0.6 copy.9
Async XLA Ops:
  0.7 0.7 copy-start

commit v8 on v7

--- a/solution.py
+++ b/solution.py
@@ -56,7 +56,7 @@
     e_hbm, source_hbm, record_hbm, shot_hbm, factor_ref, lag_hbm, out_ref,
     e_ref, source_ref, record_ref, shot_ref, lag_ref, inbuf, fin, field, sel, part, corein, two, one, three, rel_up, rel_down, from_down, from_up,
     acc, pieces, gath, xs, xb, g,
-    e_sem, lag_sem, raw_sem, chain_send, chain_recv, core_send, core_recv, x_send, x_recv, d_send, d_recv, greet_sem,
+    e_sem, lag_sem, raw_sem, chain_send, chain_recv, core_send, core_recv, x_send, x_recv, d_send, d_recv, greet_sem, token_sem,
 ):
     d = lax.axis_index("depth")
     f = lax.axis_index("freq")
@@ -196,7 +196,13 @@
             ).astype(BF16)
         return carry
 
-    two_steps(0, 0, True)
+    @pl.when(d > 0)
+    def _():
+        pl.semaphore_wait(token_sem, 1)
+
+    @pl.when(d < DEPTHS - 1)
+    def _():
+        pl.semaphore_signal(token_sem, inc=1, device_id={"depth": d + 1}, device_id_type=MESH)
 
     def greet(k, carry):
         for peer in (f, across):
@@ -206,6 +212,7 @@
         return carry
 
     lax.fori_loop(0, d, greet, 0)
+    two_steps(0, 0, True)
     lax.fori_loop(1, BATCHES // 2, two_steps, 0)
 
     mine = pl.ds(pl.multiple_of(core * ROWS, ROWS), ROWS)
@@ -440,6 +447,7 @@
             pltpu.SemaphoreType.DMA((2, DEPTHS)),
             pltpu.SemaphoreType.DMA((2, DEPTHS)),
             pltpu.SemaphoreType.REGULAR,
+            pltpu.SemaphoreType.REGULAR,
         ],
         compiler_params=pltpu.CompilerParams(
             collective_id=0, has_side_effects=True, vmem_limit_bytes=67043328 - 10400 * 1024

time: 109 us -> 109 us (level)
  no operation moved by 1% of the time
where the time goes in v8:
time: 109 us; the launch traced here: 108 us
  Pallas kernels  106 us (97%)
  local copies, waits for them, and re-layouts  1.28 us (1%)
    pallas_call x1, Pallas kernels, migrate(): pl.pallas_call(kernel, out_shape=jax.ShapeDtypeStruct((PIECE, DEPTHS, ANG...  106 us

profile of v8, /device:TPU:32, one launch (start us, length us, event | category | flops | bytes accessed | tf_op | source)
XLA Modules:
  0.0 108.4 jit_solution(9246263872589710680)
XLA Ops:
  0.7 0.0 copy-start
  0.7 0.6 copy-done
  1.3 106.4 %migrate.1 = f32[4,16,256]{2,1,0:T(8,128)S(1)} custom-call(bf16[2,1024,1024]{2,1,0:T(8,128)(2,1)} %bitcast.5, bf16[128,2,1024]{2,1,0:T(2,128)(2,1)} %bitcast.6, bf16[128,2,1024]{2,1,0:T(2,128)(2,1)} %bitcast.7, s32[1,128]{1,0:T(1,128)S(1)} %bitcast.4, f32[1]{0:T(128)S(6)} %div.4.factor_ref, s32[1024,256]{1,0:T(8,128)} %lag_hbm.1), custom_call_target="tpu_custom_call" | custom-call | tf_op jit(solution)/shard_map/migrate/pallas_call | solution.py:408
  107.7 0.6 copy.9
Async XLA Ops:
  0.7 0.7 copy-start
